TPU v7x, 256 devices: a whole 4x4x8 slice. The times are simulated.
256 devices in a mesh: expert: 32 (over y, z), mp: 8 (over x, core).
Axes of the slice: x: 4, y: 4, z: 8, core: 2. Of those that a mesh axis runs over, the one named last changes fastest.
Arguments:
- tokens: bfloat16 [4096, 3584], P('expert', 'mp'), may hold values from -6 to 6
- assignments: int32 [4096, 2], P('expert'), may hold values from 0 to 31, all different within a row; in each aligned block of 128 rows (0 to 127, 128 to 255, ...) at most 16 rows name the same one
- gate_probs: float32 [4096, 2], P('expert'), may hold values from 0.05 to 0.5
- expert_gate: bfloat16 [32, 3584, 2560], P('expert', None, 'mp'), may hold values from -0.09375 to 0.09375
- expert_up: bfloat16 [32, 3584, 2560], P('expert', None, 'mp'), may hold values from -0.09375 to 0.09375
- expert_down: bfloat16 [32, 2560, 3584], P('expert', 'mp'), may hold values from -0.125 to 0.125
- shared_gate: bfloat16 [3584, 10240], P('mp', 'expert'), may hold values from -0.09375 to 0.09375
- shared_up: bfloat16 [3584, 10240], P('mp', 'expert'), may hold values from -0.09375 to 0.09375
- shared_down_weight: bfloat16 [10240, 3584], P('expert', 'mp'), may hold values from -0.0625 to 0.0625
Outputs:
- layer_out: bfloat16 [4096, 3584], P('expert', 'mp')
Inputs may be any that keep to these rules, and one draw needn't show every extreme that they name: `assignments`: each row names 2 different experts; among the 128 rows of one index of the expert axis (aligned blocks) no expert is named more than 16 times.
All inputs are finite; a program needn't handle non-finite values.
Results may differ from a plain program's by a relative error of at most 0.0075.
Values may be sent and summed in bfloat16 or wider, within the bound.
A program may use at most 128 MiB of HBM per device.

v0:
```python
import jax
import jax.numpy as jnp
from jax import lax
from jax.sharding import Mesh
from jax.sharding import PartitionSpec as P

EXPERT = ("expert_0", "expert_1")


def laid_out(tiles, dim):
    shape = list(tiles.shape[1:])
    shape[dim] *= tiles.shape[0]
    return jnp.moveaxis(tiles, 0, dim).reshape(shape)


def from_everyone(x, axis):
    devices = lax.axis_size(axis)
    return lax.all_to_all(jnp.broadcast_to(x[None], (devices, *x.shape)), axis, 0, 0, tiled=True)


def gathered_copies(x, axis, dim):
    return laid_out(from_everyone(x, axis), dim)


def sum_by_axis(subtotal, axes):
    for axis in axes:
        subtotal = lax.psum_scatter(subtotal, axis, scatter_dimension=0, tiled=True)
    return subtotal


def cut_along(x, dim, devices):
    shape = x.shape
    tiles = x.reshape(*shape[:dim], devices, shape[dim] // devices, *shape[dim + 1 :])
    return jnp.moveaxis(tiles, dim, 0)


def sum_at_owner(x, axis, dim):
    devices = lax.axis_size(axis)
    tiles = lax.all_to_all(cut_along(x, dim, devices), axis, 0, 0, tiled=True)
    return jnp.sum(tiles, axis=0)


def split_parts(values):
    high = values.astype(jnp.bfloat16)
    low = (values - high.astype(jnp.float32)).astype(jnp.bfloat16)
    return (high, low)


def on_device(
    tokens,
    assignments,
    gate_probs,
    expert_gate,
    expert_up,
    expert_down,
    shared_gate,
    shared_up,
    shared_down_weight,
):
    experts = lax.axis_size(EXPERT)
    local_rows, chosen = assignments.shape
    capacity = min(local_rows, max(2, 2 * local_rows * chosen // experts))
    slots_all = experts * capacity
    shared_hidden_width = shared_gate.shape[1]
    joined = jnp.concatenate([shared_gate, shared_up], axis=1)
    shared_both = jnp.dot(
        lax.all_gather(tokens, EXPERT, axis=0, tiled=True),
        joined,
        preferred_element_type=jnp.float32,
    )
    share = lax.psum_scatter(shared_both, "mp", scatter_dimension=0, tiled=True)
    hidden_portion_part = (
        jax.nn.silu(share[:, :shared_hidden_width]) * share[:, shared_hidden_width:]
    ).astype(jnp.bfloat16)
    shared_hidden = gathered_copies(hidden_portion_part, "mp", 0)
    shared_result = sum_by_axis(
        jnp.dot(shared_hidden, shared_down_weight, preferred_element_type=jnp.float32), EXPERT
    )
    flat_ids = assignments.reshape(-1)
    pairs = flat_ids.shape[0]
    onehot = (jnp.arange(experts, dtype=jnp.int32)[:, None] == flat_ids[None, :]).astype(jnp.int32)
    slot_rank = jnp.sum((jnp.cumsum(onehot, axis=1) - onehot) * onehot, axis=0)
    column = flat_ids * capacity + slot_rank
    picker = (column[:, None] == jnp.arange(slots_all, dtype=jnp.int32)[None, :]).astype(
        jnp.float32
    )
    owner_row = jnp.arange(pairs, dtype=jnp.int32) // chosen
    folding = (jnp.arange(local_rows, dtype=jnp.int32)[:, None] == owner_row[None, :]).astype(
        jnp.float32
    )
    indicator = jnp.dot(folding, picker, precision=lax.Precision.HIGHEST)
    dispatch = indicator.T.astype(jnp.bfloat16)
    combine = jnp.dot(
        folding, picker * gate_probs.reshape(-1)[:, None], precision=lax.Precision.HIGHEST
    )
    combine_high, combine_low = split_parts(combine)
    weight_gate = expert_gate[0]
    weight_up = expert_up[0]
    weight_down = expert_down[0]
    outgoing = jnp.dot(dispatch, tokens, preferred_element_type=jnp.float32).astype(jnp.bfloat16)
    received = lax.all_to_all(
        outgoing.reshape(experts, capacity, -1), EXPERT, split_axis=0, concat_axis=0, tiled=True
    )
    received = received.reshape(slots_all, -1)
    portion = lax.all_gather(received, "mp", axis=1, tiled=True)
    gate_acc = jnp.dot(portion, weight_gate, preferred_element_type=jnp.float32)
    up_acc = jnp.dot(portion, weight_up, preferred_element_type=jnp.float32)
    hidden = (jax.nn.silu(gate_acc) * up_acc).astype(jnp.bfloat16)
    partial_value = jnp.dot(hidden, weight_down, preferred_element_type=jnp.float32).astype(
        jnp.bfloat16
    )
    returned = lax.all_to_all(
        partial_value.reshape(experts, capacity, -1),
        EXPERT,
        split_axis=0,
        concat_axis=0,
        tiled=True,
    )
    returned = returned.reshape(slots_all, -1)
    local_sum = jnp.dot(combine_high, returned, preferred_element_type=jnp.float32) + jnp.dot(
        combine_low, returned, preferred_element_type=jnp.float32
    )
    routed = sum_at_owner(local_sum, "mp", 1)
    return (shared_result + routed).astype(jnp.bfloat16)


def solution(mesh):
    split = Mesh(mesh.devices.reshape(4, 8, mesh.shape["mp"]), ("expert_0", "expert_1", "mp"))
    placed = (
        P(EXPERT, "mp"),
        P(EXPERT, None),
        P(EXPERT, None),
        P(EXPERT, None, "mp"),
        P(EXPERT, None, "mp"),
        P(EXPERT, "mp", None),
        P("mp", EXPERT),
        P("mp", EXPERT),
        P(EXPERT, "mp"),
    )
    return jax.shard_map(
        on_device, mesh=split, in_specs=placed, out_specs=P(EXPERT, "mp"), check_vma=False
    )
```

profile of v0, /device:TPU:7, one launch (start us, length us, event | category | flops | bytes accessed | tf_op | source)
XLA Modules:
  0.0 387.8 jit_solution(11844460795623685605)
XLA Ops:
  6.5 0.7 all-gather.3.cloned.1.call-update
  7.3 83.1 %all-gather.3.cloned.1.call-done = bf16[4096,448]{0,1:T(8,128)(2,1)} async-done(((bf16[128,448]{0,1:T(8,128)(2,1)}), bf16[4096,448]{0,1:T(8,128)(2,1)}) %all-gather.3.cloned.1.call-update) | async-done | bytes 3670032 | tf_op jit(solution)/shard_map/all_gather | solution.py:67
  90.4 9.1 %convolution_bitcast_fusion = f32[4096,640]{0,1:T(8,128)} fusion(bf16[4096,448]{0,1:T(8,128)(2,1)} %all-gather.3.cloned.1.call-done, bf16[448,320]{0,1:T(8,128)(2,1)} %param.16, bf16[448,320]{0,1:T(8,128)(2,1)} %param.15), kind=kOutput, calls=%fused_computation | convolution fusion | flops 2349957120 | bytes 14729216 | tf_op jit(solution)/shard_map/dot_general | solution.py:66
  99.6 0.6 copy-done.3
  100.7 0.6 reduce-window.6
  102.5 17.9 %all_to_all.20 = bf16[32,16,448]{2,1,0:T(8,128)(2,1)S(1)} all-to-all(bf16[32,16,448]{2,1,0:T(8,128)(2,1)S(1)} %bitcast.41), channel_id=1, replica_groups=mesh['expert_0'=4,'expert_1'=8,'mp'=8] {'expert_0','expert_1'}, dimensions={0} | all-to-all | bytes 917504 | tf_op jit(solution)/shard_map/all_to_all | solution.py:101
  120.4 1.0 copy.28
  121.5 45.0 %reduce-scatter.4.cloned.1.call-done = f32[512,640]{0,1:T(8,128)} async-done(((f32[4096,640]{0,1:T(8,128)}), f32[512,640]{0,1:T(8,128)}) %reduce-scatter.4.cloned.1.call-update) | async-done | bytes 1310736 | tf_op jit(solution)/shard_map/reduce_scatter | solution.py:71
  166.5 1.5 fusion.13
  168.2 49.6 %all_to_all.21 = bf16[8,512,320]{1,2,0:T(8,128)(2,1)S(1)} all-to-all(bf16[8,512,320]{1,2,0:T(8,128)(2,1)S(1)} %broadcast_in_dim.2), channel_id=1, replica_groups=mesh['expert_0'=4,'expert_1'=8,'mp'=8] {'mp'}, dimensions={0} | all-to-all | bytes 5242880 | tf_op jit(solution)/shard_map/all_to_all | solution.py:18
  218.1 0.6 copy-done.2
  218.8 5.1 %fusion.40 = f32[4096,448]{0,1:T(8,128)} fusion(bf16[4096,320]{0,1:T(8,128)(2,1)S(1)} %bitcast.37, bf16[320,448]{1,0:T(8,128)(2,1)S(1)} %copy-done.2), kind=kOutput, calls=%fused_computation.52 | convolution fusion | flops 1174405120 | bytes 10248192 | tf_op jit(solution)/shard_map/dot_general | solution.py:77
  223.9 4.1 %fusion.3 = f32[512,320]{0,1:T(8,128)S(1)} fusion(bf16[512,3584]{0,1:T(8,128)(2,1)} %all-gather.5.cloned.1.call-done, bf16[1,3584,320]{1,2,0:T(8,128)(2,1)} %param.12), kind=kOutput, calls=%fused_computation.6 | convolution fusion | flops 1174405120 | bytes 6619136 | tf_op jit(solution)/shard_map/dot_general | solution.py:106
  228.0 7.9 %convolution_convert_fusion = bf16[512,3584]{1,0:T(8,128)(2,1)} fusion(bf16[1,320,3584]{2,1,0:T(8,128)(2,1)S(1)} %copy-done, bf16[512,3584]{0,1:T(8,128)(2,1)} %all-gather.5.cloned.1.call-done, bf16[1,3584,320]{1,2,0:T(8,128)(2,1)} %param.13, f32[512,320]{0,1:T(8,128)S(1)} %fusion.3), kind=kOutput, calls=%fused_computation.1 | convolution fusion | flops 2351628288 | bytes 12582912 | tf_op jit(solution)/shard_map/dot_general | solution.py:109
  235.9 9.8 %all-to-all-start.2 = ((bf16[32,16,3584]{2,1,0:T(8,128)(2,1)}), bf16[32,16,3584]{2,1,0:T(8,128)(2,1)}, u32[]{:S(2)}, u32[]{:S(2)}) async-start(bf16[32,16,3584]{2,1,0:T(8,128)(2,1)} %bitcast.40), calls=%async_computation.5 | async-start | bytes 7340032 | tf_op jit(solution)/shard_map/all_to_all | solution.py:112
  245.8 94.0 %reduce-scatter.6.cloned.1.call-done = f32[1024,448]{0,1:T(8,128)} async-done(((f32[4096,448]{0,1:T(8,128)}), f32[1024,448]{0,1:T(8,128)}) %reduce-scatter.6.cloned.1.call-update) | async-done | bytes 1835024 | tf_op jit(solution)/shard_map/reduce_scatter | solution.py:27
  340.1 0.5 fusion.22
  340.5 2.7 fusion.32
  343.2 4.0 %convolution_add_fusion = f32[128,3584]{1,0:T(8,128)} fusion(f32[128,3584]{1,0:T(8,128)S(1)} %fusion.32, bf16[512,3584]{1,0:T(8,128)(2,1)} %bitcast.8, f32[128,512]{1,0:T(8,128)S(1)} %fusion.22), kind=kOutput, calls=%fused_computation.2 | convolution fusion | flops 470482944 | bytes 7602176 | tf_op jit(solution)/shard_map/dot_general | solution.py:120
  347.2 2.7 copy.29
  350.0 26.9 %all_to_all.22 = f32[8,128,448]{1,2,0:T(8,128)} all-to-all(f32[8,128,448]{1,2,0:T(8,128)} %bitcast.39), channel_id=1, replica_groups=mesh['expert_0'=4,'expert_1'=8,'mp'=8] {'mp'}, dimensions={0} | all-to-all | bytes 3670016 | tf_op jit(solution)/shard_map/all_to_all | solution.py:39
  376.9 1.6 reduce_sum.22
  378.5 1.2 reduce-scatter.8.cloned.1.call-done
  379.7 1.6 add_convert_fusion
  (37 shorter events, 2.8 us)
Async XLA Ops:
  6.5 221.4 %copy-start = (bf16[1,320,3584]{2,1,0:T(8,128)(2,1)S(1)}, bf16[1,320,3584]{2,1,0:T(8,128)(2,1)}, u32[]{:S(2)}) copy-start(bf16[1,320,3584]{2,1,0:T(8,128)(2,1)} %param.14) | copy-start | bytes 6881284
  6.5 83.9 %all-gather.3.cloned.1.call-start = ((), (), s32[]{:S(2)}) async-start(), calls=%async_computation.7 | async-start | bytes 3784704 | tf_op jit(solution)/shard_map/all_gather | solution.py:67
  7.3 159.2 %reduce-scatter.4.cloned.1.call-start = ((), (), s32[]{:S(2)}) async-start(), calls=%async_computation.8 | async-start | bytes 11796480 | tf_op jit(solution)/shard_map/reduce_scatter | solution.py:71
  99.5 0.7 copy-start.3
  99.5 2.5 copy-start.1
  99.5 124.3 %all-gather.5.cloned.1.call-start = ((), (), s32[]{:S(2)}) async-start(), calls=%async_computation.11 | async-start | bytes 4128768 | tf_op jit(solution)/shard_map/all_gather | solution.py:105
  121.4 218.3 %reduce-scatter.6.cloned.1.call-start = ((), (), s32[]{:S(2)}) async-start(), calls=%async_computation.9 | async-start | bytes 9175040 | tf_op jit(solution)/shard_map/reduce_scatter | solution.py:27
  217.8 1.0 copy-start.2
  235.9 103.9 %copy-start.4 = (f32[128,2]{0,1:T(2,128)S(1)}, f32[128,2]{0,1:T(2,128)}, u32[]{:S(2)}) copy-start(f32[128,2]{0,1:T(2,128)} %param.11) | copy-start | bytes 3076
  235.9 104.6 %all-to-all-start.2 = ((bf16[32,16,3584]{2,1,0:T(8,128)(2,1)}), bf16[32,16,3584]{2,1,0:T(8,128)(2,1)}, u32[]{:S(2)}, u32[]{:S(2)}) async-start(bf16[32,16,3584]{2,1,0:T(8,128)(2,1)} %bitcast.40), calls=%async_computation.5 | async-start | bytes 7340032 | tf_op jit(solution)/shard_map/all_to_all | solution.py:112
  245.8 133.9 %reduce-scatter.8.cloned.1.call-start = ((), (), s32[]{:S(2)}) async-start(), calls=%async_computation.10 | async-start | bytes 2064384 | tf_op jit(solution)/shard_map/reduce_scatter | solution.py:27
Sparse Core Ops, SparseCore 0:
  9.8 80.5 all-gather.2
  99.7 66.7 reduce-scatter.3
  168.3 49.5 all-gather.4
  224.0 115.7 reduce-scatter.5
  342.2 37.4 reduce-scatter.7
where the time goes:
time: 392 us; the launch traced here: 388 us
  waiting for transfers between devices  224 us (57%)
  blocking collectives  94.4 us (24%)
  matrix products  34 us (9%)
  between operations  13.3 us (3%)
  starting transfers between devices  9.99 us (3%)
  local copies, waits for them, and re-layouts  6.67 us (2%)
  other arithmetic  5.45 us (1%)
    reduce_scatter x2, waiting for transfers between devices, sum_by_axis(): subtotal = lax.psum_scatter(subtotal, axis, scatter_dimension=0, tiled=True)  95.1 us
    all_gather x1, waiting for transfers between devices, on_device(): lax.all_gather(tokens, EXPERT, axis=0, tiled=True)  83.1 us
    all_to_all x1, blocking collectives, from_everyone(): lax.all_to_all(jnp.broadcast_to(x[None], (devices, *x.shape)), axis, 0, 0...  49.6 us
    reduce_scatter x1, waiting for transfers between devices, on_device(): share = lax.psum_scatter(shared_both, 'mp', scatter_dimension=0, tiled=True)  45 us
    all_to_all x1, blocking collectives, sum_at_owner(): tiles = lax.all_to_all(cut_along(x, dim, devices), axis, 0, 0, tiled=True)  26.9 us
    all_to_all x1, blocking collectives, on_device(): lax.all_to_all(outgoing.reshape(experts, capacity, -1), EXPERT, split_axi...  17.9 us
    all_to_all x1, starting transfers between devices, on_device(): lax.all_to_all(partial_value.reshape(experts, capacity, -1), EXPERT, spli...  9.83 us
    dot_general x1, matrix products, on_device(): jnp.dot(lax.all_gather(tokens, EXPERT, axis=0, tiled=True), joined, prefe...  9.13 us
  transfers between devices with their start and end apart: 6, of which 4 were waited for; matrix products, arithmetic and copies ran while one was open for 9% of the time, Pallas kernels for 0%

commit v1 on v0

v1 whole, which is shorter than its diff:
```python
import functools
import heapq

import jax
import jax.numpy as jnp
from jax import lax
from jax.experimental import pallas as pl
from jax.experimental.pallas import tpu as pltpu
from jax.sharding import PartitionSpec as P

MESH = pl.DeviceIdType.MESH
BF = jnp.bfloat16
F32 = jnp.float32
NY, NZ, NX, NM = 4, 8, 4, 8
BLOCK = 128
PIECE = 16
FEAT = 3584
LOCAL = 448
WIDE = FEAT + 128
SLOTS = 64
SPLIT = 1536
RATE = 80e3
HOP = 1.8


def cut(lo, n):
    first = (n // 128) // 2 * 128
    return (lo, first), (lo + first, n - first)


def ring(index, offset, size):
    return lax.rem(index + (offset + size) % size, size)


class Place:
    def __init__(self):
        e = lax.axis_index("expert")
        self.m = lax.axis_index("mp")
        self.y, self.z = lax.div(e, NZ), lax.rem(e, NZ)
        self.x, self.c = lax.div(self.m, 2), lax.rem(self.m, 2)

    def at(self, axis, d):
        y, z, m = self.y, self.z, self.m
        if axis == "y":
            y = ring(y, d, NY)
        elif axis == "z":
            z = ring(z, d, NZ)
        elif axis == "x":
            m = ring(self.x, d, NX) * 2 + self.c
        else:
            m = self.x * 2 + 1 - self.c
        return (y * NZ + z, m)


def greet(peers, extra=()):
    barrier = pltpu.get_barrier_semaphore()
    for device in peers:
        pl.semaphore_signal(barrier, inc=1, device_id=device, device_id_type=MESH)
    for condition, device in extra:

        @pl.when(condition)
        def _():
            pl.semaphore_signal(barrier, inc=1, device_id=device, device_id_type=MESH)

    return barrier


class Wire:
    def __init__(self, place, send_sem, recv_sem):
        self.place, self.send_sem, self.recv_sem = place, send_sem, recv_sem
        self.count, self.queue, self.sent, self.free, self.now = 0, [], [], {}, 0.0

    def send(self, axis, d, src, dst, size, then):
        k = self.count
        self.count += 1
        copy = pltpu.make_async_remote_copy(
            src_ref=src,
            dst_ref=dst,
            send_sem=self.send_sem.at[k],
            recv_sem=self.recv_sem.at[k],
            device_id=self.place.at(axis, d),
            device_id_type=MESH,
        )
        copy.start()
        self.sent.append(copy)
        begin = max(self.now, self.free.get((axis, d), 0.0))
        end = begin + size * 2 / RATE
        self.free[(axis, d)] = end
        heapq.heappush(self.queue, (end + HOP, k, copy, then))

    def run(self):
        while self.queue:
            when, _, copy, then = heapq.heappop(self.queue)
            self.now = max(self.now, when)
            copy.wait_recv()
            if then is not None:
                then()

    def drain(self):
        for copy in self.sent:
            copy.wait_send()


def gather_kernel(
    tok_ref, wgu_ref, wd_ref, x_ref, gu_ref, down_ref, pieces, own, send_sem, recv_sem, part_send, part_recv, local_sem
):
    p = Place()
    y, z, m = p.y, p.z, p.m
    mine = z == m
    sources = [(y * NZ + m, q) for q in range(NM)]
    targets = [(y * NZ + r, z) for r in range(NZ)]
    neighbours = [p.at(a, d) for a, d in (("x", 1), ("x", -1), ("y", 1), ("y", -1), ("z", 1), ("z", -1), ("c", 1))]
    barrier = greet(
        neighbours, [(jnp.logical_not(jnp.logical_and(mine, m == q)), sources[q]) for q in range(NM)]
    )
    pl.semaphore_wait(barrier, len(neighbours) + NM - mine.astype(jnp.int32))

    for r in range(NZ):
        src = tok_ref.at[pl.ds(r * PIECE, PIECE), :]
        away = jnp.logical_not(jnp.logical_and(mine, z == r))

        @pl.when(away)
        def _():
            pltpu.make_async_remote_copy(
                src_ref=src,
                dst_ref=pieces.at[m],
                send_sem=part_send.at[r],
                recv_sem=part_recv.at[m],
                device_id=targets[r],
                device_id_type=MESH,
            ).start()

        @pl.when(jnp.logical_not(away))
        def _():
            pltpu.make_async_copy(src, pieces.at[m], part_recv.at[m]).start()

    keep_gu = pltpu.make_async_copy(wgu_ref, gu_ref.at[m], local_sem.at[0])
    keep_gu.start()
    keep_down = pltpu.make_async_copy(wd_ref, down_ref.at[m], local_sem.at[1])
    keep_down.start()

    wire = Wire(p, send_sem, recv_sem)

    def weights(own_ref, out, rows, width):
        size = rows * width * 2

        def block(xo, partner, lo, n):
            c = 1 - p.c if partner else p.c
            return out.at[ring(p.x, xo, NX) * 2 + c, pl.ds(lo, n), :]

        def share(xo, lo, n):
            wire.send("c", 1, block(xo, False, lo, n), block(xo, False, lo, n), size * n // rows, None)

        def arrived(d, xo, lo, n):
            def then():
                if abs(xo) == 1:
                    low, high = cut_rows(lo, n)
                    a, k = low if d == 1 else high
                    wire.send(
                        "x", d, block(xo, False, a, k), block(xo, False, a, k), size * k // rows, arrived(d, xo - d, a, k)
                    )
                share(xo, lo, n)

            return then

        for d in (1, -1):
            wire.send("x", d, own_ref, out.at[m], size, arrived(d, -d, 0, rows))
        wire.send("c", 1, own_ref, out.at[m], size, None)

    def cut_rows(lo, n):
        first = (n // 16) // 2 * 16
        return (lo, first), (lo + first, n - first)

    weights(wgu_ref, gu_ref, LOCAL, 640)
    weights(wd_ref, down_ref, 320, 512)

    for q in range(NM):
        pltpu.make_async_copy(pieces.at[q], pieces.at[q], part_recv.at[q]).wait()
    parts = [pieces[q][:, :LOCAL] for q in range(NM)]
    tail = jnp.concatenate([pieces[0][:, LOCAL:], jnp.zeros((PIECE, 64), BF)], axis=1)
    own[...] = jnp.concatenate(parts + [tail], axis=1)

    keep = pltpu.make_async_copy(own, x_ref.at[z, y], local_sem.at[2])
    keep.start()
    wire.now = 6.0

    def block(zo, yo, lo, n):
        return x_ref.at[ring(z, zo, NZ), ring(y, yo, NY), :, pl.ds(lo, n)]

    def forward(axis, d, zo, yo, lo, n, src=None):
        dst = block(zo, yo, lo, n)
        wire.send(axis, d, dst if src is None else src, dst, PIECE * n * 2, arrived(axis, d, zo, yo, lo, n))

    def arrived(axis, d, zo, yo, lo, n):
        if axis == "z":
            zo -= d
            dist, far = abs(zo), 4
        else:
            yo -= d
            dist, far = abs(yo), 2

        def then():
            if dist < far - 1:
                forward(axis, d, zo, yo, lo, n)
            elif dist == far - 1:
                low, high = cut(lo, n)
                forward(axis, d, zo, yo, *(low if d == 1 else high))
            if axis == "y" and lo < SPLIT:
                for s in (1, -1):
                    forward("z", s, zo, yo, lo, n)
            if axis == "z" and lo >= SPLIT:
                for s in (1, -1):
                    forward("y", s, zo, yo, lo, n)

        return then

    for axes, lo, n in ((("y", "z"), 0, SPLIT), (("z", "y"), SPLIT, WIDE - SPLIT)):
        for axis in axes:
            for d in (1, -1):
                forward(axis, d, 0, 0, lo, n, own.at[:, pl.ds(lo, n)])
    wire.run()
    keep_gu.wait()
    keep_down.wait()
    keep.wait()
    for r in range(NZ):

        @pl.when(jnp.logical_not(jnp.logical_and(mine, z == r)))
        def _():
            pltpu.make_async_copy(
                tok_ref.at[pl.ds(r * PIECE, PIECE), :], tok_ref.at[pl.ds(r * PIECE, PIECE), :], part_send.at[r]
            ).wait()

    wire.drain()


def spec(space):
    return pl.BlockSpec(memory_space=space)


VM = pltpu.VMEM
ANY = pl.ANY


def params(number):
    return pltpu.CompilerParams(collective_id=number, has_side_effects=True, vmem_limit_bytes=48 * 2**20)


def gather(tok, wgu, wd):
    return pl.pallas_call(
        gather_kernel,
        name="gather",
        out_shape=(
            jax.ShapeDtypeStruct((NZ, NY, PIECE, WIDE), BF),
            jax.ShapeDtypeStruct((NM, LOCAL, 640), BF),
            jax.ShapeDtypeStruct((NM, 320, LOCAL), BF),
        ),
        in_specs=[spec(VM)] * 3,
        out_specs=[spec(ANY)] * 3,
        scratch_shapes=[
            pltpu.VMEM((NM, PIECE, 512), BF),
            pltpu.VMEM((PIECE, WIDE), BF),
            pltpu.SemaphoreType.DMA((112,)),
            pltpu.SemaphoreType.DMA((112,)),
            pltpu.SemaphoreType.DMA((NZ,)),
            pltpu.SemaphoreType.DMA((NM,)),
            pltpu.SemaphoreType.DMA((3,)),
        ],
        compiler_params=params(0),
    )(tok, wgu, wd)


def slots_kernel(s_ref, out_ref, send_sem, recv_sem, local_sem):
    p = Place()
    neighbours = [p.at("x", 1), p.at("x", -1), p.at("c", 1)]
    barrier = greet(neighbours)
    pl.semaphore_wait(barrier, 3)
    wire = Wire(p, send_sem, recv_sem)
    keep = pltpu.make_async_copy(s_ref, out_ref.at[p.m], local_sem)
    keep.start()

    def block(xo, lo, n):
        return out_ref.at[ring(p.x, xo, NX) * 2 + p.c, :, pl.ds(lo, n)]

    def forward(axis, d, xo, lo, n, src=None):
        dst = block(xo, lo, n)
        then = arrived(d, xo - d, lo, n) if axis == "x" else None
        wire.send(axis, d, dst if src is None else src, dst, SLOTS * n * 2, then)

    def arrived(d, xo, lo, n):
        def then():
            if abs(xo) == 1:
                low, high = cut(lo, n)
                forward("x", d, xo, *(low if d == 1 else high))
            forward("c", 1, xo, lo, n)

        return then

    for d in (1, -1):
        for lo, n in cut(0, FEAT)[:: d]:
            forward("x", d, 0, lo, n, s_ref.at[:, pl.ds(lo, n)])
    forward("c", 1, 0, 0, FEAT, s_ref)
    wire.run()
    keep.wait()
    wire.drain()


def gather_slots(s):
    return pl.pallas_call(
        slots_kernel,
        name="gather_slots",
        out_shape=jax.ShapeDtypeStruct((NM, SLOTS, FEAT), BF),
        in_specs=[spec(VM)],
        out_specs=spec(VM),
        scratch_shapes=[
            pltpu.SemaphoreType.DMA((24,)),
            pltpu.SemaphoreType.DMA((24,)),
            pltpu.SemaphoreType.DMA,
        ],
        compiler_params=params(1),
    )(s)


def sum_slots_kernel(r_ref, out_ref, from_pair, from_x, held, send_sem, recv_sem):
    p = Place()
    neighbours = [p.at("x", 1), p.at("x", -1), p.at("c", 1)]
    barrier = greet(neighbours)
    pl.semaphore_wait(barrier, 3)
    wire = Wire(p, send_sem, recv_sem)
    low, high = cut(0, FEAT)

    def mine(xo):
        return r_ref[ring(p.x, xo, NX) * 2 + p.c].astype(F32)

    landed = {1: None, -1: None}

    def far():
        held[2] = (mine(2) + from_pair[2].astype(F32)).astype(BF)
        for d, (lo, n) in ((1, low), (-1, high)):
            at = pl.ds(lo, n)
            wire.send("x", d, held.at[2, :, at], from_x.at[0 if d == 1 else 1, :, at], SLOTS * n * 2, passed(d, lo, n))

    ready = {}

    def near(d):
        def then():
            ready[(d, "pair")] = True
            onward(d)

        return then

    def passed(d, lo, n):
        def then():
            ready[(d, "far")] = (lo, n)
            onward(d)

        return then

    def onward(d):
        if (d, "pair") not in ready or (d, "far") not in ready:
            return
        slot = 1 if d == 1 else 3
        lo, n = ready[(d, "far")]
        k = 0 if d == 1 else 1
        total = mine(d) + from_pair[slot].astype(F32)
        held[slot] = total.astype(BF)
        at = pl.ds(lo, n)
        held[slot, :, at] = (total[:, lo : lo + n] + from_x[k, :, at].astype(F32)).astype(BF)
        wire.send("x", d, held.at[slot], from_x.at[2 + k], SLOTS * FEAT * 2, None)

    after = {2: far, 1: near(1), 3: near(-1), 0: None}
    for xo in (2, 1, 3, 0):
        src = r_ref.at[ring(p.x, xo, NX) * 2 + 1 - p.c]
        wire.send("c", 1, src, from_pair.at[xo], SLOTS * FEAT, after[xo])
    wire.run()
    out_ref[...] = mine(0) + from_pair[0].astype(F32) + from_x[2].astype(F32) + from_x[3].astype(F32)
    wire.drain()


def sum_slots(r):
    return pl.pallas_call(
        sum_slots_kernel,
        name="sum_slots",
        out_shape=jax.ShapeDtypeStruct((SLOTS, FEAT), F32),
        in_specs=[spec(VM)],
        out_specs=spec(VM),
        scratch_shapes=[
            pltpu.VMEM((NX, SLOTS, FEAT), BF),
            pltpu.VMEM((4, SLOTS, FEAT), BF),
            pltpu.VMEM((4, SLOTS, FEAT), BF),
            pltpu.SemaphoreType.DMA((16,)),
            pltpu.SemaphoreType.DMA((16,)),
        ],
        compiler_params=params(2),
    )(r)


def reduce_kernel(
    in_ref, out_ref, held, z_in, y_in, pieces, send_sem, recv_sem, part_send, part_recv
):
    p = Place()
    y, z, m = p.y, p.z, p.m
    mine = z == m
    sources = [(y * NZ + r, z) for r in range(NZ)]
    targets = [(y * NZ + m, q) for q in range(NM)]
    neighbours = [p.at(a, d) for a, d in (("y", 1), ("y", -1), ("z", 1), ("z", -1))]
    barrier = greet(
        neighbours, [(jnp.logical_not(jnp.logical_and(mine, z == r)), sources[r]) for r in range(NZ)]
    )
    pl.semaphore_wait(barrier, len(neighbours) + NM - mine.astype(jnp.int32))
    wire = Wire(p, send_sem, recv_sem)

    def index(zo, yo):
        return ring(z, zo, NZ), ring(y, yo, NY)

    sizes = {"z": NZ, "y": NY}
    inbox = {"z": z_in, "y": y_in}

    class Chain:
        def __init__(self, axis, other, lo, n, second, done):
            self.axis, self.other, self.lo, self.n = axis, other, lo, n
            self.second, self.done, self.left = second, done, 2
            self.far = sizes[axis] // 2
            self.ready = {}

        def where(self, o):
            return (o, self.other) if self.axis == "z" else (self.other, o)

        def mailbox(self, d, left, lo, n):
            zo, yo = self.where(0)
            k = (0 if d == 1 else 1) * self.far + left
            other = self.other % (NY if self.axis == "z" else NZ)
            return inbox[self.axis].at[k, other, :, pl.ds(lo, n)]

        def source(self, o, lo, n):
            a, b = index(*self.where(o))
            ref = held if self.second else in_ref
            return ref.at[a, b, :, pl.ds(lo, n)]

        def have(self, o):
            self.ready[o % sizes[self.axis]] = True
            if o % sizes[self.axis] == self.far:
                low, high = cut(self.lo, self.n)
                for d, (lo, n) in ((1, low), (-1, high)):
                    wire.send(
                        self.axis,
                        d,
                        self.source(self.far, lo, n),
                        self.mailbox(d, self.far - 1, lo, n),
                        PIECE * n * 2,
                        self.arrived(d, self.far - 1, lo, n),
                    )
            for d in (1, -1):
                self.step(d, o * d % sizes[self.axis])

        def arrived(self, d, left, lo, n):
            def then():
                self.ready[(d, left)] = (lo, n)
                self.step(d, left)

            return then

        def step(self, d, left):
            size = sizes[self.axis]
            o = d * left
            if left == 0 or left >= self.far:
                if left == 0:
                    self.finish()
                return
            if (d, left) not in self.ready or o % size not in self.ready:
                return
            lo, n = self.ready[(d, left)]
            a, b = index(*self.where(o))
            at = pl.ds(lo, n)
            base = held if self.second else in_ref
            if (lo, n) != (self.lo, self.n) and not self.second:
                rest = [c for c in cut(self.lo, self.n) if c != (lo, n)][0]
                held[a, b, :, pl.ds(*rest)] = in_ref[a, b, :, pl.ds(*rest)]
            total = base[a, b, :, at].astype(F32) + self.mailbox(d, left, lo, n)[...].astype(F32)
            held[a, b, :, at] = total.astype(BF)
            wire.send(
                self.axis,
                d,
                held.at[a, b, :, pl.ds(self.lo, self.n)],
                self.mailbox(d, left - 1, self.lo, self.n),
                PIECE * self.n * 2,
                self.arrived(d, left - 1, self.lo, self.n),
            )

        def finish(self):
            if (1, 0) not in self.ready or (-1, 0) not in self.ready or 0 not in self.ready or self.left == 0:
                return
            self.left = 0
            a, b = index(*self.where(0))
            at = pl.ds(self.lo, self.n)
            base = held if self.second else in_ref
            total = base[a, b, :, at].astype(F32)
            for d in (1, -1):
                total = total + self.mailbox(d, 0, self.lo, self.n)[...].astype(F32)
            if not self.second:
                held[a, b, :, at] = total.astype(BF)
            self.done(total)

    last = {}

    def plan(first, second, lo, n):
        def store(total):
            last[lo] = total

        final = Chain(second, 0, lo, n, True, store)
        far = sizes[second] // 2
        offsets = sorted(range(sizes[second]), key=lambda o: (-min(o, sizes[second] - o), o))
        chains = []
        for o in offsets:
            signed = o if o <= far else o - sizes[second]
            chains.append(Chain(first, signed, lo, n, False, lambda total, s=signed: final.have(s)))
        return chains

    groups = [plan("z", "y", 0, SPLIT), plan("y", "z", SPLIT, FEAT - SPLIT)]
    for group in groups:
        for chain in group:
            far = chain.far
            order = [far] + [s * d for d in range(far - 1, 0, -1) for s in (1, -1)] + [0]
            for o in order:
                chain.have(o)
    wire.run()
    whole = jnp.concatenate([last[0], last[SPLIT]], axis=1).astype(BF)
    for q in range(NM):
        pieces[q] = whole[:, q * LOCAL : (q + 1) * LOCAL]
    rows = pl.ds(pl.multiple_of(z * PIECE, PIECE), PIECE)
    for q in range(NM):
        away = jnp.logical_not(jnp.logical_and(mine, m == q))

        @pl.when(away)
        def _():
            pltpu.make_async_remote_copy(
                src_ref=pieces.at[q],
                dst_ref=out_ref.at[rows, :],
                send_sem=part_send.at[q],
                recv_sem=part_recv.at[z],
                device_id=targets[q],
                device_id_type=MESH,
            ).start()

        @pl.when(jnp.logical_not(away))
        def _():
            pltpu.make_async_copy(pieces.at[q], out_ref.at[rows, :], part_recv.at[z]).start()

    for r in range(NZ):
        pltpu.make_async_copy(pieces.at[r], pieces.at[r], part_recv.at[r]).wait()
    for q in range(NM):

        @pl.when(jnp.logical_not(jnp.logical_and(mine, m == q)))
        def _():
            pltpu.make_async_copy(pieces.at[q], pieces.at[q], part_send.at[q]).wait()

    wire.drain()


def reduce_out(partial):
    return pl.pallas_call(
        reduce_kernel,
        name="reduce_out",
        out_shape=jax.ShapeDtypeStruct((BLOCK, LOCAL), BF),
        in_specs=[spec(VM)],
        out_specs=spec(VM),
        scratch_shapes=[
            pltpu.VMEM((NZ, NY, PIECE, FEAT), BF),
            pltpu.VMEM((2 * (NZ // 2), NY, PIECE, FEAT), BF),
            pltpu.VMEM((2 * (NY // 2), NZ, PIECE, FEAT), BF),
            pltpu.VMEM((NM, PIECE, LOCAL), BF),
            pltpu.SemaphoreType.DMA((96,)),
            pltpu.SemaphoreType.DMA((96,)),
            pltpu.SemaphoreType.DMA((NM,)),
            pltpu.SemaphoreType.DMA((NZ,)),
        ],
        compiler_params=params(3),
    )(partial)


def dot(a, b):
    return jnp.dot(a, b, preferred_element_type=F32)


def rounded(v):
    return lax.reduce_precision(v, 8, 7)


def thirds(v):
    high = rounded(v)
    middle = rounded(v - high)
    return high, middle, v - high - middle


def on_device(tokens, assignments, gate_probs, expert_gate, expert_up, expert_down, shared_gate, shared_up, shared_down):
    me = lax.axis_index("expert").astype(F32)
    split = [part for k in range(2) for part in thirds(gate_probs[:, k : k + 1])]
    meta = jnp.concatenate([assignments.astype(F32)] + split + [jnp.zeros((BLOCK, 56), F32)], axis=1)
    tok = jnp.concatenate([tokens, meta.astype(BF)], axis=1)
    x, gu, down = gather(tok, jnp.concatenate([shared_gate, shared_up], axis=1), shared_down)
    x = x.reshape(NZ * NY * PIECE, WIDE)
    info = x[:, FEAT : FEAT + 8].astype(F32)
    x = x[:, :FEAT]
    rows = x.shape[0]

    named = (info[:, 0:2] == me).astype(F32)
    hit = named[:, 0] + named[:, 1]
    weight = named[:, 0] * (info[:, 2] + info[:, 3] + info[:, 4]) + named[:, 1] * (info[:, 5] + info[:, 6] + info[:, 7])
    t = jnp.arange(rows, dtype=jnp.int32)
    group = (t // PIECE) % NY
    before = ((t[:, None] < t[None, :]) & (group[:, None] == group[None, :])).astype(BF)
    rank = dot(hit.astype(BF)[None, :], before)[0]
    slot = jnp.where(hit > 0, group * 16 + rank.astype(jnp.int32), -1)
    place = slot[None, :] == jnp.arange(SLOTS, dtype=jnp.int32)[:, None]
    picked = dot(place.astype(BF), x).astype(BF)

    routed_in = gather_slots(picked).reshape(NM * SLOTS, FEAT)
    shared_act = dot(x, gu.reshape(FEAT, 640))
    shared_hidden = (jax.nn.silu(shared_act[:, :320]) * shared_act[:, 320:]).astype(BF)
    shared_out = dot(shared_hidden, jnp.moveaxis(down, 0, 1).reshape(320, FEAT))

    gate = dot(routed_in, expert_gate[0])
    up = dot(routed_in, expert_up[0])
    hidden = (jax.nn.silu(gate) * up).astype(BF)
    routed = dot(hidden, expert_down[0]).astype(BF)
    total = sum_slots(routed.reshape(NM, SLOTS, FEAT))

    scale = jnp.sum(place.astype(F32) * weight[None, :], axis=1)
    value = total * scale[:, None]
    back = place.astype(BF).T
    partial = shared_out + dot(back, value.astype(BF))
    return reduce_out(partial.astype(BF).reshape(NZ, NY, PIECE, FEAT))


def solution(mesh):
    placed = (
        P("expert", "mp"),
        P("expert", None),
        P("expert", None),
        P("expert", None, "mp"),
        P("expert", None, "mp"),
        P("expert", "mp", None),
        P("mp", "expert"),
        P("mp", "expert"),
        P("expert", "mp"),
    )
    return jax.shard_map(on_device, mesh=mesh, in_specs=placed, out_specs=P("expert", "mp"), check_vma=False)
```

time: 392 us -> 187 us (0.48)
  waiting for transfers between devices: 224 us -> 0 us
  Pallas kernels: 0 us -> 140 us
  blocking collectives: 94.4 us -> 0 us
  between operations: 13.3 us -> 0.18 us
  local copies, waits for them, and re-layouts: 6.67 us -> 18.9 us
  starting transfers between devices: 9.99 us -> 0 us
  matrix products: 34 us -> 25.7 us
  other arithmetic: 5.45 us -> 1.25 us
    pallas_call x0 -> x4, Pallas kernels: none -> 140 us  [the longest x1 51.2 us: gather(): pl.pallas_call(gather_kernel, name='gather', out_shape=(jax.ShapeDtypeStr...]
    reduce_scatter x3 -> x0, waiting for transfers between devices: 140 us -> none  [the longest x2 95.1 us: sum_by_axis(): subtotal = lax.psum_scatter(subtotal, axis, scatter_dimension=0, tiled=True)]
    all_to_all x3 -> x0, blocking collectives: 94.4 us -> none  [the longest x1 49.6 us: from_everyone(): lax.all_to_all(jnp.broadcast_to(x[None], (devices, *x.shape)), axis, 0, 0...]
    all_gather x2 -> x0, waiting for transfers between devices: 83.1 us -> none  [the longest x1 83.1 us: on_device(): lax.all_gather(tokens, EXPERT, axis=0, tiled=True)]
    all_to_all x1 -> x0, starting transfers between devices: 9.83 us -> none  [on_device(): lax.all_to_all(partial_value.reshape(experts, capacity, -1), EXPERT, spli...]
    dot_general x9 -> x7, matrix products: 34 us -> 25.7 us  [dot(): return jnp.dot(a, b, preferred_element_type=F32)]
    unnamed x12 -> x22, local copies, waits for them, and re-layouts: 1.45 us -> 7.33 us
    reshape x2 -> x1, local copies, waits for them, and re-layouts: 1.33 us -> 5.65 us  [on_device(): shared_out = dot(shared_hidden, jnp.moveaxis(down, 0, 1).reshape(320, FEAT))]
  transfers between devices with their start and end apart: 6 -> 0, of which waited for: 4 -> 0; matrix products, arithmetic and copies ran while one was open for 9% -> 0% of each run, Pallas kernels for 0% -> 0%
where the time goes in v1:
time: 187 us; the launch traced here: 186 us
  Pallas kernels  140 us (75%)
  matrix products  25.7 us (14%)
  local copies, waits for them, and re-layouts  18.9 us (10%)
    pallas_call x1, Pallas kernels, gather(): pl.pallas_call(gather_kernel, name='gather', out_shape=(jax.ShapeDtypeStr...  51.2 us
    pallas_call x1, Pallas kernels, reduce_out(): pl.pallas_call(reduce_kernel, name='reduce_out', out_shape=jax.ShapeDtype...  44.8 us
    dot_general x7, matrix products, dot(): return jnp.dot(a, b, preferred_element_type=F32)  25.7 us
    pallas_call x1, Pallas kernels, sum_slots(): pl.pallas_call(sum_slots_kernel, name='sum_slots', out_shape=jax.ShapeDty...  22.4 us
    pallas_call x1, Pallas kernels, gather_slots(): pl.pallas_call(slots_kernel, name='gather_slots', out_shape=jax.ShapeDtyp...  21.8 us
    unnamed x22, local copies, waits for them, and re-layouts  7.33 us
    reshape x1, local copies, waits for them, and re-layouts, on_device(): shared_out = dot(shared_hidden, jnp.moveaxis(down, 0, 1).reshape(320, FEAT))  5.65 us

profile of v1, /device:TPU:7, one launch (start us, length us, event | category | flops | bytes accessed | tf_op | source)
XLA Modules:
  0.0 186.3 jit_solution(12899780961405754061)
XLA Ops:
  0.0 0.8 convert_convert_fusion
  0.8 0.8 fusion.39
  2.0 1.0 copy.52
  3.0 0.2 concatenate.9.tok_ref
  3.2 1.2 copy.54
  4.4 1.2 copy.55
  5.6 0.2 pad_maximum_fusion.wgu_ref
  5.8 51.2 %gather.1 = (bf16[8,4,16,3712]{3,2,1,0:T(8,128)(2,1)}, bf16[8,448,640]{2,1,0:T(8,128)(2,1)}, bf16[8,320,448]{2,1,0:T(8,128)(2,1)S(1)}) custom-call(bf16[128,512]{1,0:T(8,128)(2,1)S(1)} %concatenate.9.tok_ref, bf16[448,640]{1,0:T(8,128)(2,1)S(1)} %pad_maximum_fusion.wgu_ref, bf16[320,448]{1,0:T(8,128)(2,1)S(1)} %copy-done.5), custom_call_target="tpu_custom_call" | custom-call | tf_op jit(solution)/shard_map/gather/pallas_call | solution.py:249
  57.1 8.4 %fusion.1 = f32[512,640]{1,0:T(8,128)} fusion(bf16[3584,640]{1,0:T(8,128)(2,1)} %bitcast.38, bf16[512,3712]{1,0:T(8,128)(2,1)} %bitcast.34), kind=kOutput, calls=%fused_computation.4 | convolution fusion | flops 2348810240 | bytes 9568256 | tf_op jit(solution)/shard_map/dot_general | solution.py:581
  65.5 0.9 slice.65
  66.5 0.3 fusion.15
  66.8 3.0 %convolution_convert_fusion.1.s_ref = bf16[64,3584]{1,0:T(8,128)(2,1)S(1)} fusion(bf16[512,3712]{1,0:T(8,128)(2,1)} %bitcast.36, s32[512]{0:T(512)S(1)} %add_select_fusion.2), kind=kOutput, calls=%fused_computation.2 | convolution fusion | flops 235143168 | bytes 4130816 | tf_op jit(solution)/shard_map/dot_general | solution.py:581
  70.0 3.0 %copy.56 = bf16[320,8,448]{2,1,0:T(8,128)(2,1)} copy(bf16[320,8,448]{2,0,1:T(8,128)(2,1)S(1)} %bitcast.32) | data formatting | bytes 4587520 | tf_op jit(solution)/shard_map/transpose | solution.py:619
  72.9 5.6 %reshape.139 = bf16[320,3584]{1,0:T(8,128)(2,1)} reshape(bf16[320,8,448]{2,1,0:T(8,128)(2,1)} %copy.56) | data formatting | bytes 4587520 | tf_op jit(solution)/shard_map/reshape | solution.py:619
  78.6 21.8 %gather_slots.1 = bf16[8,64,3584]{2,1,0:T(8,128)(2,1)S(1)} custom-call(bf16[64,3584]{1,0:T(8,128)(2,1)S(1)} %convolution_convert_fusion.1.s_ref), custom_call_target="tpu_custom_call" | custom-call | tf_op jit(solution)/shard_map/gather_slots/pallas_call | solution.py:308
  100.4 1.8 copy-done.1
  102.2 2.1 %fusion.6 = f32[512,320]{1,0:T(8,128)S(1)} fusion(bf16[512,3584]{1,0:T(8,128)(2,1)S(1)} %bitcast.29, bf16[1,3584,320]{1,2,0:T(8,128)(2,1)S(1)} %copy-done.8), kind=kOutput, calls=%fused_computation.9 | convolution fusion | flops 1174405120 | bytes 6619136 | tf_op jit(solution)/shard_map/dot_general | solution.py:581
  104.3 8.6 %convolution_convert_fusion = bf16[512,3584]{1,0:T(8,128)(2,1)} fusion(bf16[1,320,3584]{2,1,0:T(8,128)(2,1)S(1)} %copy-done, bf16[512,3584]{1,0:T(8,128)(2,1)} %bitcast.30, bf16[1,3584,320]{1,2,0:T(8,128)(2,1)} %param.13, f32[512,320]{1,0:T(8,128)S(1)} %fusion.6), kind=kOutput, calls=%fused_computation.1 | convolution fusion | flops 2351628288 | bytes 12582912 | tf_op jit(solution)/shard_map/dot_general | solution.py:581
  112.9 2.0 %copy-done.2 = bf16[512,3584]{1,0:T(8,128)(2,1)S(1)} copy-done((bf16[512,3584]{1,0:T(8,128)(2,1)S(1)}, bf16[512,3584]{1,0:T(8,128)(2,1)}, u32[]{:S(2)}) %copy-start.2) | copy-done | bytes 3670040
  114.9 22.4 %sum_slots.1 = f32[64,3584]{1,0:T(8,128)S(1)} custom-call(bf16[8,64,3584]{2,1,0:T(8,128)(2,1)S(1)} %bitcast.31), custom_call_target="tpu_custom_call" | custom-call | tf_op jit(solution)/shard_map/sum_slots/pallas_call | solution.py:380
  137.3 2.1 %fusion.23 = f32[512,3584]{1,0:T(8,128)S(1)} fusion(bf16[320,3584]{1,0:T(8,128)(2,1)S(1)} %copy-done.6, f32[512,640]{1,0:T(8,128)S(1)} %copy-done.7), kind=kOutput, calls=%fused_computation.23 | convolution fusion | flops 1175388160 | bytes 11206656 | tf_op jit(solution)/shard_map/dot_general | solution.py:581
  139.4 1.2 add_convert_fusion
  140.7 44.8 %reduce_out.1 = bf16[128,448]{1,0:T(8,128)(2,1)S(1)} custom-call(bf16[8,4,16,3584]{3,2,1,0:T(8,128)(2,1)S(1)} %bitcast.28), custom_call_target="tpu_custom_call" | custom-call | tf_op jit(solution)/shard_map/reduce_out/pallas_call | solution.py:560
  185.5 0.8 copy.61
  (29 shorter events, 0.7 us)
Async XLA Ops:
  0.0 104.3 %copy-start = (bf16[1,320,3584]{2,1,0:T(8,128)(2,1)S(1)}, bf16[1,320,3584]{2,1,0:T(8,128)(2,1)}, u32[]{:S(2)}) copy-start(bf16[1,320,3584]{2,1,0:T(8,128)(2,1)} %param.14) | copy-start | bytes 6881284
  0.0 5.8 %copy-start.5 = (bf16[320,448]{1,0:T(8,128)(2,1)S(1)}, bf16[320,448]{1,0:T(8,128)(2,1)}, u32[]{:S(2)}) copy-start(bf16[320,448]{1,0:T(8,128)(2,1)} %wd_ref.1) | copy-start | bytes 860164
  57.1 8.4 %copy-start.3 = (bf16[8,320,448]{2,1,0:T(8,128)(2,1)}, bf16[8,320,448]{2,1,0:T(8,128)(2,1)S(1)}, u32[]{:S(2)}) copy-start(bf16[8,320,448]{2,1,0:T(8,128)(2,1)S(1)} %get-tuple-element.10) | copy-start | bytes 6881284
  66.4 3.5 %copy-start.4 = (bf16[8,320,448]{2,1,0:T(8,128)(2,1)S(1)}, bf16[8,320,448]{2,1,0:T(8,128)(2,1)}, u32[]{:S(2)}) copy-start(bf16[8,320,448]{2,1,0:T(8,128)(2,1)} %copy-done.3) | copy-start | bytes 6881284
  78.6 23.6 %copy-start.8 = (bf16[1,3584,320]{1,2,0:T(8,128)(2,1)S(1)}, bf16[1,3584,320]{1,2,0:T(8,128)(2,1)}, u32[]{:S(2)}) copy-start(bf16[1,3584,320]{1,2,0:T(8,128)(2,1)} %param.12) | copy-start | bytes 6881284
  100.4 1.8 copy-start.1
  112.9 2.0 %copy-start.2 = (bf16[512,3584]{1,0:T(8,128)(2,1)S(1)}, bf16[512,3584]{1,0:T(8,128)(2,1)}, u32[]{:S(2)}) copy-start(bf16[512,3584]{1,0:T(8,128)(2,1)} %convolution_convert_fusion) | copy-start | bytes 11010052
  114.9 22.4 %copy-start.6 = (bf16[320,3584]{1,0:T(8,128)(2,1)S(1)}, bf16[320,3584]{1,0:T(8,128)(2,1)}, u32[]{:S(2)}) copy-start(bf16[320,3584]{1,0:T(8,128)(2,1)} %reshape.139) | copy-start | bytes 6881284
  114.9 22.4 %copy-start.7 = (f32[512,640]{1,0:T(8,128)S(1)}, f32[512,640]{1,0:T(8,128)}, u32[]{:S(2)}) copy-start(f32[512,640]{1,0:T(8,128)} %fusion.1) | copy-start | bytes 3932164

commit v2 on v1

--- a/solution.py
+++ b/solution.py
@@ -1,4 +1,3 @@
-import functools
 import heapq
 
 import jax
@@ -19,8 +18,9 @@
 WIDE = FEAT + 128
 SLOTS = 64
 SPLIT = 1536
-RATE = 80e3
-HOP = 1.8
+RATE = 92e3
+HOP = 2.6
+LATE = 4.0
 
 
 def cut(lo, n):
@@ -69,8 +69,9 @@
     def __init__(self, place, send_sem, recv_sem):
         self.place, self.send_sem, self.recv_sem = place, send_sem, recv_sem
         self.count, self.queue, self.sent, self.free, self.now = 0, [], [], {}, 0.0
-
-    def send(self, axis, d, src, dst, size, then):
+        self.count_other = 0
+
+    def send(self, axis, d, src, dst, size, then, late=0.0):
         k = self.count
         self.count += 1
         copy = pltpu.make_async_remote_copy(
@@ -86,13 +87,18 @@
         begin = max(self.now, self.free.get((axis, d), 0.0))
         end = begin + size * 2 / RATE
         self.free[(axis, d)] = end
-        heapq.heappush(self.queue, (end + HOP, k, copy, then))
+        heapq.heappush(self.queue, (end + HOP + late, k, copy, then))
+
+    def push(self, when, then):
+        self.count_other -= 1
+        heapq.heappush(self.queue, (when, self.count_other, None, then))
 
     def run(self):
         while self.queue:
             when, _, copy, then = heapq.heappop(self.queue)
             self.now = max(self.now, when)
-            copy.wait_recv()
+            if copy is not None:
+                copy.wait_recv()
             if then is not None:
                 then()
 
@@ -144,35 +150,39 @@
     def weights(own_ref, out, rows, width):
         size = rows * width * 2
 
-        def block(xo, partner, lo, n):
-            c = 1 - p.c if partner else p.c
-            return out.at[ring(p.x, xo, NX) * 2 + c, pl.ds(lo, n), :]
+        def block(xo, lo, n):
+            return out.at[ring(p.x, xo, NX) * 2 + p.c, pl.ds(lo, n), :]
+
+        half = cut_rows(0, rows)
 
         def share(xo, lo, n):
-            wire.send("c", 1, block(xo, False, lo, n), block(xo, False, lo, n), size * n // rows, None)
+            at = block(xo, lo, n)
+            wire.send("c", 1, at, at, size * n // rows // 4, None, 2 * LATE)
 
         def arrived(d, xo, lo, n):
             def then():
-                if abs(xo) == 1:
-                    low, high = cut_rows(lo, n)
-                    a, k = low if d == 1 else high
-                    wire.send(
-                        "x", d, block(xo, False, a, k), block(xo, False, a, k), size * k // rows, arrived(d, xo - d, a, k)
-                    )
+                if abs(xo) == 1 and (lo, n) == half[0 if d == 1 else 1]:
+                    at = block(xo, lo, n)
+                    wire.send("x", d, at, at, size * n // rows, arrived(d, xo - d, lo, n), LATE)
                 share(xo, lo, n)
 
             return then
 
-        for d in (1, -1):
-            wire.send("x", d, own_ref, out.at[m], size, arrived(d, -d, 0, rows))
-        wire.send("c", 1, own_ref, out.at[m], size, None)
+        def begin(first):
+            for d in (1, -1):
+                lo, n = half[0 if (d == 1) == first else 1]
+                src = own_ref.at[pl.ds(lo, n), :]
+                wire.send("x", d, src, block(0, lo, n), size * n // rows, arrived(d, -d, lo, n), LATE)
+            if first:
+                wire.send("c", 1, own_ref, out.at[m], size // 4, None, 2 * LATE)
+
+        return begin
 
     def cut_rows(lo, n):
         first = (n // 16) // 2 * 16
         return (lo, first), (lo + first, n - first)
 
-    weights(wgu_ref, gu_ref, LOCAL, 640)
-    weights(wd_ref, down_ref, 320, 512)
+    sends = [weights(wgu_ref, gu_ref, LOCAL, 640), weights(wd_ref, down_ref, 320, 512)]
 
     for q in range(NM):
         pltpu.make_async_copy(pieces.at[q], pieces.at[q], part_recv.at[q]).wait()
@@ -183,6 +193,9 @@
     keep = pltpu.make_async_copy(own, x_ref.at[z, y], local_sem.at[2])
     keep.start()
     wire.now = 6.0
+    for first in (True, False):
+        for begin in sends:
+            begin(first)
 
     def block(zo, yo, lo, n):
         return x_ref.at[ring(z, zo, NZ), ring(y, yo, NY), :, pl.ds(lo, n)]
@@ -259,8 +272,8 @@
         scratch_shapes=[
             pltpu.VMEM((NM, PIECE, 512), BF),
             pltpu.VMEM((PIECE, WIDE), BF),
-            pltpu.SemaphoreType.DMA((112,)),
-            pltpu.SemaphoreType.DMA((112,)),
+            pltpu.SemaphoreType.DMA((128,)),
+            pltpu.SemaphoreType.DMA((128,)),
             pltpu.SemaphoreType.DMA((NZ,)),
             pltpu.SemaphoreType.DMA((NM,)),
             pltpu.SemaphoreType.DMA((3,)),
@@ -269,82 +282,126 @@
     )(tok, wgu, wd)
 
 
-def slots_kernel(s_ref, out_ref, send_sem, recv_sem, local_sem):
+ROWS = 2 * SLOTS
+OFFSETS = (0, 1, 3, 2)
+
+
+def experts_kernel(
+    s_ref, back_ref, scale_ref, x_hbm, gu_hbm, wd_hbm, eg_hbm, eu_hbm, ed_hbm, out_ref,
+    shared, value, rows, eg, eu, ed, xs, gu, wd, wide, part, from_pair, from_x, held, send_sem, recv_sem, local_sem, load_sem,
+):
     p = Place()
+    loads = [
+        pltpu.make_async_copy(src, dst, load_sem.at[k])
+        for k, (src, dst) in enumerate(
+            ((eg_hbm, eg), (eu_hbm, eu), (ed_hbm, ed), (wd_hbm, wd), (gu_hbm, gu), (x_hbm, xs))
+        )
+    ]
+    for load in loads:
+        load.start()
     neighbours = [p.at("x", 1), p.at("x", -1), p.at("c", 1)]
     barrier = greet(neighbours)
     pl.semaphore_wait(barrier, 3)
     wire = Wire(p, send_sem, recv_sem)
-    keep = pltpu.make_async_copy(s_ref, out_ref.at[p.m], local_sem)
+    wire.now = 3.0
+    keep = pltpu.make_async_copy(s_ref, rows.at[p.m], local_sem)
     keep.start()
+    low, high = cut(0, FEAT)
 
     def block(xo, lo, n):
-        return out_ref.at[ring(p.x, xo, NX) * 2 + p.c, :, pl.ds(lo, n)]
-
-    def forward(axis, d, xo, lo, n, src=None):
-        dst = block(xo, lo, n)
-        then = arrived(d, xo - d, lo, n) if axis == "x" else None
-        wire.send(axis, d, dst if src is None else src, dst, SLOTS * n * 2, then)
-
-    def arrived(d, xo, lo, n):
+        return rows.at[ring(p.x, xo, NX) * 2 + p.c, :, pl.ds(lo, n)]
+
+    def base(xo):
+        return ring(p.x, xo, NX) * 2
+
+    missing = {0: 1, 1: 4, 3: 4, 2: 4}
+
+    def landed(xo):
         def then():
-            if abs(xo) == 1:
-                low, high = cut(lo, n)
-                forward("x", d, xo, *(low if d == 1 else high))
-            forward("c", 1, xo, lo, n)
+            missing[xo] -= 1
+            if missing[xo] == 0:
+                routed(xo)
 
         return then
 
-    for d in (1, -1):
-        for lo, n in cut(0, FEAT)[:: d]:
-            forward("x", d, 0, lo, n, s_ref.at[:, pl.ds(lo, n)])
-    forward("c", 1, 0, 0, FEAT, s_ref)
-    wire.run()
-    keep.wait()
-    wire.drain()
-
-
-def gather_slots(s):
-    return pl.pallas_call(
-        slots_kernel,
-        name="gather_slots",
-        out_shape=jax.ShapeDtypeStruct((NM, SLOTS, FEAT), BF),
-        in_specs=[spec(VM)],
-        out_specs=spec(VM),
-        scratch_shapes=[
-            pltpu.SemaphoreType.DMA((24,)),
-            pltpu.SemaphoreType.DMA((24,)),
-            pltpu.SemaphoreType.DMA,
-        ],
-        compiler_params=params(1),
-    )(s)
-
-
-def sum_slots_kernel(r_ref, out_ref, from_pair, from_x, held, send_sem, recv_sem):
-    p = Place()
-    neighbours = [p.at("x", 1), p.at("x", -1), p.at("c", 1)]
-    barrier = greet(neighbours)
-    pl.semaphore_wait(barrier, 3)
-    wire = Wire(p, send_sem, recv_sem)
-    low, high = cut(0, FEAT)
-
-    def mine(xo):
-        return r_ref[ring(p.x, xo, NX) * 2 + p.c].astype(F32)
-
-    landed = {1: None, -1: None}
-
-    def far():
-        held[2] = (mine(2) + from_pair[2].astype(F32)).astype(BF)
-        for d, (lo, n) in ((1, low), (-1, high)):
-            at = pl.ds(lo, n)
-            wire.send("x", d, held.at[2, :, at], from_x.at[0 if d == 1 else 1, :, at], SLOTS * n * 2, passed(d, lo, n))
+    def share(xo, lo, n):
+        wire.send("c", 1, block(xo, lo, n), block(xo, lo, n), SLOTS * n, landed(xo % NX))
+
+    def moved(d, xo, lo, n):
+        def then():
+            if abs(xo) == 1 and (lo, n) == (low if d == 1 else high):
+                dst = block(xo, lo, n)
+                wire.send("x", d, dst, dst, SLOTS * n * 2, moved(d, xo - d, lo, n))
+                if d == -1:
+                    wire.push(wire.now, lambda: filler(1, 1))
+            share(xo, lo, n)
+            landed(xo % NX)()
+
+        return then
+
+    for first in (True, False):
+        for d in (1, -1):
+            lo, n = low if (d == 1) == first else high
+            wire.send("x", d, s_ref.at[:, pl.ds(lo, n)], block(0, lo, n), SLOTS * n * 2, moved(d, -d, lo, n))
+        if first:
+            wire.send("c", 1, s_ref, rows.at[p.m], SLOTS * FEAT // 2, landed(0))
+
+    def turned(a, b):
+        return lax.dot_general(a, b, (((1,), (1,)), ((), ())), preferred_element_type=F32)
+
+    def routed(xo):
+        if xo == 0:
+            keep.wait()
+            for load in loads[:3]:
+                load.wait()
+        chunk = rows[pl.ds(base(xo), 2)].reshape(ROWS, FEAT)
+        hidden = (jax.nn.silu(turned(chunk, eg[...])) * turned(chunk, eu[...])).astype(BF)
+        part[xo] = dot(hidden, ed[...]).astype(BF).reshape(2, SLOTS, FEAT)
+        wire.now += 2.5
+        wire.send("c", 1, part.at[xo, 1 - p.c], from_pair.at[xo], SLOTS * FEAT // 2, paired(xo))
+        if xo == 0:
+            filler(0, 1)
+        if xo == 2:
+            wire.push(wire.now + 5.0, lambda: filler(2, 2))
+
+    def filler(start, count):
+        if start == 0:
+            for load in loads[3:]:
+                load.wait()
+            wide[...] = jnp.concatenate([wd[q] for q in range(NM)], axis=1)
+
+        def body(i, carry):
+            at = pl.ds(pl.multiple_of(i * ROWS, ROWS), ROWS)
+            both = dot(xs[at, :FEAT], gu[...])
+            hidden = (jax.nn.silu(both[:, :320]) * both[:, 320:640]).astype(BF)
+            shared[at, :] = dot(hidden, wide[...])
+            return carry
+
+        lax.fori_loop(start, start + count, body, 0)
+        wire.now += 2.5 * count
+
+    def own_sum(xo):
+        return part[xo, p.c].astype(F32) + from_pair[xo].astype(F32)
 
     ready = {}
 
-    def near(d):
+    def paired(xo):
         def then():
-            ready[(d, "pair")] = True
-            onward(d)
+            if xo == 0:
+                return
+            held[xo] = own_sum(xo).astype(BF)
+            for d in (1, -1):
+                lo, n = low if d == 1 else high
+                k = 0 if d == 1 else 1
+                if xo == 2:
+                    at = pl.ds(lo, n)
+                    wire.send("x", d, held.at[2, :, at], from_x.at[k, :, at], SLOTS * n * 2, passed(d, lo, n))
+                elif xo == d % NX:
+                    lo, n = high if d == 1 else low
+                    at = pl.ds(lo, n)
+                    wire.send("x", d, held.at[xo, :, at], from_x.at[2 + k, :, at], SLOTS * n * 2, None)
+                    ready[(d, "pair")] = True
+                    onward(d)
 
         return then
 
@@ -358,40 +415,57 @@
     def onward(d):
         if (d, "pair") not in ready or (d, "far") not in ready:
             return
-        slot = 1 if d == 1 else 3
+        slot = d % NX
         lo, n = ready[(d, "far")]
         k = 0 if d == 1 else 1
-        total = mine(d) + from_pair[slot].astype(F32)
-        held[slot] = total.astype(BF)
         at = pl.ds(lo, n)
-        held[slot, :, at] = (total[:, lo : lo + n] + from_x[k, :, at].astype(F32)).astype(BF)
-        wire.send("x", d, held.at[slot], from_x.at[2 + k], SLOTS * FEAT * 2, None)
-
-    after = {2: far, 1: near(1), 3: near(-1), 0: None}
-    for xo in (2, 1, 3, 0):
-        src = r_ref.at[ring(p.x, xo, NX) * 2 + 1 - p.c]
-        wire.send("c", 1, src, from_pair.at[xo], SLOTS * FEAT, after[xo])
+        total = part[slot, p.c, :, at].astype(F32) + from_pair[slot, :, at].astype(F32) + from_x[k, :, at].astype(F32)
+        held[slot, :, at] = total.astype(BF)
+        wire.send("x", d, held.at[slot, :, at], from_x.at[2 + k, :, at], SLOTS * n * 2, None)
+
     wire.run()
-    out_ref[...] = mine(0) + from_pair[0].astype(F32) + from_x[2].astype(F32) + from_x[3].astype(F32)
+    total = own_sum(0) + from_x[2].astype(F32) + from_x[3].astype(F32)
+    value[...] = (total * scale_ref[...]).astype(BF)
+
+    def combine(i, carry):
+        at = pl.ds(pl.multiple_of(i * ROWS, ROWS), ROWS)
+        out_ref[at, :] = (shared[at, :] + dot(back_ref[at, :], value[...])).astype(BF)
+        return carry
+
+    lax.fori_loop(0, 4, combine, 0)
     wire.drain()
 
 
-def sum_slots(r):
+def experts(s, back, scale, x, gu, wd, eg, eu, ed):
+    slots = pltpu.VMEM((NX, SLOTS, FEAT), BF)
     return pl.pallas_call(
-        sum_slots_kernel,
-        name="sum_slots",
-        out_shape=jax.ShapeDtypeStruct((SLOTS, FEAT), F32),
-        in_specs=[spec(VM)],
+        experts_kernel,
+        name="experts",
+        out_shape=jax.ShapeDtypeStruct((4 * BLOCK, FEAT), BF),
+        in_specs=[spec(VM)] * 3 + [spec(ANY)] * 6,
         out_specs=spec(VM),
         scratch_shapes=[
-            pltpu.VMEM((NX, SLOTS, FEAT), BF),
-            pltpu.VMEM((4, SLOTS, FEAT), BF),
-            pltpu.VMEM((4, SLOTS, FEAT), BF),
-            pltpu.SemaphoreType.DMA((16,)),
-            pltpu.SemaphoreType.DMA((16,)),
+            pltpu.VMEM((4 * BLOCK, FEAT), F32),
+            pltpu.VMEM((SLOTS, FEAT), BF),
+            pltpu.VMEM((NM, SLOTS, FEAT), BF),
+            pltpu.VMEM((320, FEAT), BF),
+            pltpu.VMEM((320, FEAT), BF),
+            pltpu.VMEM((320, FEAT), BF),
+            pltpu.VMEM((4 * BLOCK, WIDE), BF),
+            pltpu.VMEM((FEAT, 640), BF),
+            pltpu.VMEM((NM, 320, LOCAL), BF),
+            pltpu.VMEM((320, FEAT), BF),
+            pltpu.VMEM((NX, 2, SLOTS, FEAT), BF),
+            slots,
+            slots,
+            slots,
+            pltpu.SemaphoreType.DMA((32,)),
+            pltpu.SemaphoreType.DMA((32,)),
+            pltpu.SemaphoreType.DMA,
+            pltpu.SemaphoreType.DMA((6,)),
         ],
-        compiler_params=params(2),
-    )(r)
+        compiler_params=params(1),
+    )(s, back, scale, x, gu, wd, eg, eu, ed)
 
 
 def reduce_kernel(
@@ -597,9 +671,9 @@
     meta = jnp.concatenate([assignments.astype(F32)] + split + [jnp.zeros((BLOCK, 56), F32)], axis=1)
     tok = jnp.concatenate([tokens, meta.astype(BF)], axis=1)
     x, gu, down = gather(tok, jnp.concatenate([shared_gate, shared_up], axis=1), shared_down)
-    x = x.reshape(NZ * NY * PIECE, WIDE)
-    info = x[:, FEAT : FEAT + 8].astype(F32)
-    x = x[:, :FEAT]
+    wide_x = x.reshape(NZ * NY * PIECE, WIDE)
+    info = wide_x[:, FEAT : FEAT + 8].astype(F32)
+    x = wide_x[:, :FEAT]
     rows = x.shape[0]
 
     named = (info[:, 0:2] == me).astype(F32)
@@ -613,22 +687,20 @@
     place = slot[None, :] == jnp.arange(SLOTS, dtype=jnp.int32)[:, None]
     picked = dot(place.astype(BF), x).astype(BF)
 
-    routed_in = gather_slots(picked).reshape(NM * SLOTS, FEAT)
-    shared_act = dot(x, gu.reshape(FEAT, 640))
-    shared_hidden = (jax.nn.silu(shared_act[:, :320]) * shared_act[:, 320:]).astype(BF)
-    shared_out = dot(shared_hidden, jnp.moveaxis(down, 0, 1).reshape(320, FEAT))
-
-    gate = dot(routed_in, expert_gate[0])
-    up = dot(routed_in, expert_up[0])
-    hidden = (jax.nn.silu(gate) * up).astype(BF)
-    routed = dot(hidden, expert_down[0]).astype(BF)
-    total = sum_slots(routed.reshape(NM, SLOTS, FEAT))
-
     scale = jnp.sum(place.astype(F32) * weight[None, :], axis=1)
-    value = total * scale[:, None]
-    back = place.astype(BF).T
-    partial = shared_out + dot(back, value.astype(BF))
-    return reduce_out(partial.astype(BF).reshape(NZ, NY, PIECE, FEAT))
+    back = slot[:, None] == jnp.arange(SLOTS, dtype=jnp.int32)[None, :]
+    partial = experts(
+        picked,
+        back.astype(BF),
+        scale[:, None],
+        wide_x,
+        gu.reshape(FEAT, 640),
+        down,
+        jnp.swapaxes(expert_gate[0], 0, 1),
+        jnp.swapaxes(expert_up[0], 0, 1),
+        expert_down[0],
+    )
+    return reduce_out(partial.reshape(NZ, NY, PIECE, FEAT))
 
 
 def solution(mesh):

time: 187 us -> 161 us (0.86)
  matrix products: 25.7 us -> 3.24 us
  local copies, waits for them, and re-layouts: 18.9 us -> 9.32 us
  Pallas kernels: 140 us -> 145 us
  other arithmetic: 1.25 us -> 3.43 us
    dot_general x7 -> x2, matrix products: 25.7 us -> 3.24 us  [dot(): return jnp.dot(a, b, preferred_element_type=F32)]
    reshape x1 -> x0, local copies, waits for them, and re-layouts: 5.65 us -> none  [on_device(): shared_out = dot(shared_hidden, jnp.moveaxis(down, 0, 1).reshape(320, FEAT))]
    pallas_call x2 -> x1, Pallas kernels: 44.2 us -> 49.6 us  [experts(): pl.pallas_call(experts_kernel, name='experts', out_shape=jax.ShapeDtypeSt...]
    transpose x1 -> x0, local copies, waits for them, and re-layouts: 2.99 us -> none  [on_device(): shared_out = dot(shared_hidden, jnp.moveaxis(down, 0, 1).reshape(320, FEAT))]
    unnamed x22 -> x13, local copies, waits for them, and re-layouts: 7.33 us -> 7.01 us
where the time goes in v2:
time: 161 us
  Pallas kernels  145 us (90%)
  local copies, waits for them, and re-layouts  9.32 us (6%)
  other arithmetic  3.43 us (2%)
  matrix products  3.24 us (2%)
    pallas_call x1, Pallas kernels, experts(): pl.pallas_call(experts_kernel, name='experts', out_shape=jax.ShapeDtypeSt...  49.6 us
    pallas_call x1, Pallas kernels, gather(): pl.pallas_call(gather_kernel, name='gather', out_shape=(jax.ShapeDtypeStr...  49.6 us
    pallas_call x1, Pallas kernels, reduce_out(): pl.pallas_call(reduce_kernel, name='reduce_out', out_shape=jax.ShapeDtype...  45.8 us
    unnamed x13, local copies, waits for them, and re-layouts  7.01 us
    dot_general x2, matrix products, dot(): return jnp.dot(a, b, preferred_element_type=F32)  3.24 us

profile of v2, /device:TPU:7, one launch (start us, length us, event | category | flops | bytes accessed | tf_op | source)
XLA Modules:
  0.0 161.2 jit_solution(13486732049805016994)
XLA Ops:
  0.0 0.7 convert_convert_fusion
  0.7 0.8 fusion.17
  1.5 0.1 copy.47
  1.9 1.0 copy.46
  2.9 0.2 concatenate.9.tok_ref
  3.1 1.2 copy.48
  4.3 1.2 copy.49
  5.5 0.2 pad_maximum_fusion.wgu_ref
  5.7 49.6 %gather.1 = (bf16[8,4,16,3712]{3,2,1,0:T(8,128)(2,1)}, bf16[8,448,640]{2,1,0:T(8,128)(2,1)}, bf16[8,320,448]{2,1,0:T(8,128)(2,1)S(1)}) custom-call(bf16[128,512]{1,0:T(8,128)(2,1)S(1)} %concatenate.9.tok_ref, bf16[448,640]{1,0:T(8,128)(2,1)S(1)} %pad_maximum_fusion.wgu_ref, bf16[320,448]{1,0:T(8,128)(2,1)S(1)} %copy-done.4), custom_call_target="tpu_custom_call" | custom-call | tf_op jit(solution)/shard_map/gather/pallas_call | solution.py:262
  55.3 1.5 copy-done.1
  56.9 0.9 slice_convert_fusion
  57.8 0.6 fusion.8
  58.5 0.2 convert_reduce_fusion
  58.7 0.3 fusion.2
  59.0 0.2 copy.50
  59.2 0.2 select_reduce_fusion
  59.4 0.1 reduce
  59.6 0.1 select_reduce_fusion.1
  59.8 0.1 fusion.10.back_ref
  60.0 2.9 %convolution_convert_fusion.s_ref = bf16[64,3584]{1,0:T(8,128)(2,1)S(1)} fusion(bf16[512,3712]{1,0:T(8,128)(2,1)} %bitcast.19, s32[512]{0:T(512)S(1)} %broadcast_select_fusion), kind=kOutput, calls=%fused_computation | convolution fusion | flops 235143168 | bytes 4130816 | tf_op jit(solution)/shard_map/dot_general | solution.py:655
  62.9 49.6 %experts.1 = bf16[512,3584]{1,0:T(8,128)(2,1)} custom-call(bf16[64,3584]{1,0:T(8,128)(2,1)S(1)} %convolution_convert_fusion.s_ref, bf16[512,64]{1,0:T(8,128)(2,1)S(1)} %fusion.10.back_ref, f32[64,1]{1,0:T(8,128)S(1)} %copy.51.scale_ref, bf16[512,3712]{1,0:T(8,128)(2,1)} %bitcast.20, bf16[3584,640]{1,0:T(8,128)(2,1)} %bitcast.17, ...), custom_call_target="tpu_custom_call" | custom-call | tf_op jit(solution)/shard_map/experts/pallas_call | solution.py:441
  112.6 2.0 %copy-done = bf16[512,3584]{1,0:T(8,128)(2,1)S(1)} copy-done((bf16[512,3584]{1,0:T(8,128)(2,1)S(1)}, bf16[512,3584]{1,0:T(8,128)(2,1)}, u32[]{:S(2)}) %copy-start) | copy-done | bytes 3670040
  114.6 45.8 %reduce_out.1 = bf16[128,448]{1,0:T(8,128)(2,1)S(1)} custom-call(bf16[8,4,16,3584]{3,2,1,0:T(8,128)(2,1)S(1)} %bitcast.14), custom_call_target="tpu_custom_call" | custom-call | tf_op jit(solution)/shard_map/reduce_out/pallas_call | solution.py:634
  160.4 0.8 copy.52
  (18 shorter events, 0.4 us)
Async XLA Ops:
  0.0 5.7 %copy-start.4 = (bf16[320,448]{1,0:T(8,128)(2,1)S(1)}, bf16[320,448]{1,0:T(8,128)(2,1)}, u32[]{:S(2)}) copy-start(bf16[320,448]{1,0:T(8,128)(2,1)} %wd_ref.1) | copy-start | bytes 860164
  55.3 1.6 copy-start.1
  58.5 4.4 %copy-start.2 = (bf16[1,3584,320]{1,2,0:T(8,128)(2,1)S(1)}, bf16[1,3584,320]{1,2,0:T(8,128)(2,1)}, u32[]{:S(2)}) copy-start(bf16[1,3584,320]{1,2,0:T(8,128)(2,1)} %param.12) | copy-start | bytes 6881284
  59.8 3.1 %copy-start.3 = (bf16[1,3584,320]{1,2,0:T(8,128)(2,1)S(1)}, bf16[1,3584,320]{1,2,0:T(8,128)(2,1)}, u32[]{:S(2)}) copy-start(bf16[1,3584,320]{1,2,0:T(8,128)(2,1)} %param.13) | copy-start | bytes 6881284
  112.6 2.0 %copy-start = (bf16[512,3584]{1,0:T(8,128)(2,1)S(1)}, bf16[512,3584]{1,0:T(8,128)(2,1)}, u32[]{:S(2)}) copy-start(bf16[512,3584]{1,0:T(8,128)(2,1)} %experts.1) | copy-start | bytes 11010052

commit v3 on v2

--- a/solution.py
+++ b/solution.py
@@ -108,7 +108,8 @@
 
 
 def gather_kernel(
-    tok_ref, wgu_ref, wd_ref, x_ref, gu_ref, down_ref, pieces, own, send_sem, recv_sem, part_send, part_recv, local_sem
+    tok_t_ref, ids_ref, probs_ref, gate_t_ref, up_t_ref, wd_ref, x_ref, gu_ref, down_ref,
+    tok_t, tok_ref, wgu_t, wgu_ref, pieces, own, send_sem, recv_sem, part_send, part_recv, local_sem
 ):
     p = Place()
     y, z, m = p.y, p.z, p.m
@@ -119,6 +120,13 @@
     barrier = greet(
         neighbours, [(jnp.logical_not(jnp.logical_and(mine, m == q)), sources[q]) for q in range(NM)]
     )
+    probs = probs_ref[...]
+    high = probs.astype(BF).astype(F32)
+    middle = (probs - high).astype(BF).astype(F32)
+    meta = [ids_ref[...].astype(F32), high, middle, probs - high - middle]
+    tok_t[pl.ds(0, LOCAL), :] = tok_t_ref[...]
+    tok_t[pl.ds(LOCAL, 64), :] = jnp.concatenate(meta + [jnp.zeros((56, BLOCK), F32)], axis=0).astype(BF)
+    tok_ref[...] = tok_t[...].T
     pl.semaphore_wait(barrier, len(neighbours) + NM - mine.astype(jnp.int32))
 
     for r in range(NZ):
@@ -140,6 +148,9 @@
         def _():
             pltpu.make_async_copy(src, pieces.at[m], part_recv.at[m]).start()
 
+    wgu_t[pl.ds(0, 320), pl.ds(0, LOCAL)] = gate_t_ref[...]
+    wgu_t[pl.ds(320, 320), pl.ds(0, LOCAL)] = up_t_ref[...]
+    wgu_ref[...] = wgu_t[...].T[:LOCAL, :]
     keep_gu = pltpu.make_async_copy(wgu_ref, gu_ref.at[m], local_sem.at[0])
     keep_gu.start()
     keep_down = pltpu.make_async_copy(wd_ref, down_ref.at[m], local_sem.at[1])
@@ -254,11 +265,11 @@
 ANY = pl.ANY
 
 
-def params(number):
-    return pltpu.CompilerParams(collective_id=number, has_side_effects=True, vmem_limit_bytes=48 * 2**20)
-
-
-def gather(tok, wgu, wd):
+def params(number, mib):
+    return pltpu.CompilerParams(collective_id=number, has_side_effects=True, vmem_limit_bytes=mib * 2**20)
+
+
+def gather(tok_t, ids, probs, gate_t, up_t, wd):
     return pl.pallas_call(
         gather_kernel,
         name="gather",
@@ -267,9 +278,13 @@
             jax.ShapeDtypeStruct((NM, LOCAL, 640), BF),
             jax.ShapeDtypeStruct((NM, 320, LOCAL), BF),
         ),
-        in_specs=[spec(VM)] * 3,
-        out_specs=[spec(ANY)] * 3,
+        in_specs=[spec(VM)] * 6,
+        out_specs=[spec(pltpu.HBM)] * 3,
         scratch_shapes=[
+            pltpu.VMEM((512, BLOCK), BF),
+            pltpu.VMEM((BLOCK, 512), BF),
+            pltpu.VMEM((640, 512), BF),
+            pltpu.VMEM((LOCAL, 640), BF),
             pltpu.VMEM((NM, PIECE, 512), BF),
             pltpu.VMEM((PIECE, WIDE), BF),
             pltpu.SemaphoreType.DMA((128,)),
@@ -278,8 +293,8 @@
             pltpu.SemaphoreType.DMA((NM,)),
             pltpu.SemaphoreType.DMA((3,)),
         ],
-        compiler_params=params(0),
-    )(tok, wgu, wd)
+        compiler_params=params(0, 59),
+    )(tok_t, ids, probs, gate_t, up_t, wd)
 
 
 ROWS = 2 * SLOTS
@@ -287,20 +302,22 @@
 
 
 def experts_kernel(
-    s_ref, back_ref, scale_ref, x_hbm, gu_hbm, wd_hbm, eg_hbm, eu_hbm, ed_hbm, out_ref,
-    shared, value, rows, eg, eu, ed, xs, gu, wd, wide, part, from_pair, from_x, held, send_sem, recv_sem, local_sem, load_sem,
+    place_ref, back_ref, scale_ref, x_hbm, gu_hbm, wd_hbm, eg_hbm, eu_hbm, ed_hbm, out_ref,
+    done, s_ref, shared, value, rows, eg, eu, ed, xs, gu, wd, wide, part, from_pair, from_x, held, send_sem, recv_sem, local_sem, load_sem,
 ):
     p = Place()
     loads = [
         pltpu.make_async_copy(src, dst, load_sem.at[k])
         for k, (src, dst) in enumerate(
-            ((eg_hbm, eg), (eu_hbm, eu), (ed_hbm, ed), (wd_hbm, wd), (gu_hbm, gu), (x_hbm, xs))
+            ((x_hbm, xs), (eg_hbm, eg), (eu_hbm, eu), (ed_hbm, ed), (wd_hbm, wd), (gu_hbm, gu))
         )
     ]
     for load in loads:
         load.start()
     neighbours = [p.at("x", 1), p.at("x", -1), p.at("c", 1)]
     barrier = greet(neighbours)
+    loads[0].wait()
+    s_ref[...] = dot(place_ref[...], xs[:, :FEAT]).astype(BF)
     pl.semaphore_wait(barrier, 3)
     wire = Wire(p, send_sem, recv_sem)
     wire.now = 3.0
@@ -352,7 +369,7 @@
     def routed(xo):
         if xo == 0:
             keep.wait()
-            for load in loads[:3]:
+            for load in loads[1:4]:
                 load.wait()
         chunk = rows[pl.ds(base(xo), 2)].reshape(ROWS, FEAT)
         hidden = (jax.nn.silu(turned(chunk, eg[...])) * turned(chunk, eu[...])).astype(BF)
@@ -366,7 +383,7 @@
 
     def filler(start, count):
         if start == 0:
-            for load in loads[3:]:
+            for load in loads[4:]:
                 load.wait()
             wide[...] = jnp.concatenate([wd[q] for q in range(NM)], axis=1)
 
@@ -429,22 +446,28 @@
 
     def combine(i, carry):
         at = pl.ds(pl.multiple_of(i * ROWS, ROWS), ROWS)
-        out_ref[at, :] = (shared[at, :] + dot(back_ref[at, :], value[...])).astype(BF)
+        done[at, :] = (shared[at, :] + dot(back_ref[at, :], value[...])).astype(BF)
+        pltpu.make_async_copy(done.at[at, :], out_ref.at[at, :], load_sem.at[i]).start()
         return carry
 
     lax.fori_loop(0, 4, combine, 0)
     wire.drain()
-
-
-def experts(s, back, scale, x, gu, wd, eg, eu, ed):
+    for i in range(4):
+        at = pl.ds(i * ROWS, ROWS)
+        pltpu.make_async_copy(done.at[at, :], out_ref.at[at, :], load_sem.at[i]).wait()
+
+
+def experts(place, back, scale, x, gu, wd, eg, eu, ed):
     slots = pltpu.VMEM((NX, SLOTS, FEAT), BF)
     return pl.pallas_call(
         experts_kernel,
         name="experts",
         out_shape=jax.ShapeDtypeStruct((4 * BLOCK, FEAT), BF),
         in_specs=[spec(VM)] * 3 + [spec(ANY)] * 6,
-        out_specs=spec(VM),
+        out_specs=spec(ANY),
         scratch_shapes=[
+            pltpu.VMEM((4 * BLOCK, FEAT), BF),
+            pltpu.VMEM((SLOTS, FEAT), BF),
             pltpu.VMEM((4 * BLOCK, FEAT), F32),
             pltpu.VMEM((SLOTS, FEAT), BF),
             pltpu.VMEM((NM, SLOTS, FEAT), BF),
@@ -464,16 +487,18 @@
             pltpu.SemaphoreType.DMA,
             pltpu.SemaphoreType.DMA((6,)),
         ],
-        compiler_params=params(1),
-    )(s, back, scale, x, gu, wd, eg, eu, ed)
+        compiler_params=params(1, 54),
+    )(place, back, scale, x, gu, wd, eg, eu, ed)
 
 
 def reduce_kernel(
-    in_ref, out_ref, held, z_in, y_in, pieces, send_sem, recv_sem, part_send, part_recv
+    in_hbm, out_ref, in_ref, held, z_in, y_in, pieces, load_sem, send_sem, recv_sem, part_send, part_recv
 ):
     p = Place()
     y, z, m = p.y, p.z, p.m
     mine = z == m
+    load = pltpu.make_async_copy(in_hbm, in_ref, load_sem)
+    load.start()
     sources = [(y * NZ + r, z) for r in range(NZ)]
     targets = [(y * NZ + m, q) for q in range(NM)]
     neighbours = [p.at(a, d) for a, d in (("y", 1), ("y", -1), ("z", 1), ("z", -1))]
@@ -481,6 +506,7 @@
         neighbours, [(jnp.logical_not(jnp.logical_and(mine, z == r)), sources[r]) for r in range(NZ)]
     )
     pl.semaphore_wait(barrier, len(neighbours) + NM - mine.astype(jnp.int32))
+    load.wait()
     wire = Wire(p, send_sem, recv_sem)
 
     def index(zo, yo):
@@ -635,19 +661,21 @@
         reduce_kernel,
         name="reduce_out",
         out_shape=jax.ShapeDtypeStruct((BLOCK, LOCAL), BF),
-        in_specs=[spec(VM)],
+        in_specs=[spec(ANY)],
         out_specs=spec(VM),
         scratch_shapes=[
+            pltpu.VMEM((NZ, NY, PIECE, FEAT), BF),
             pltpu.VMEM((NZ, NY, PIECE, FEAT), BF),
             pltpu.VMEM((2 * (NZ // 2), NY, PIECE, FEAT), BF),
             pltpu.VMEM((2 * (NY // 2), NZ, PIECE, FEAT), BF),
             pltpu.VMEM((NM, PIECE, LOCAL), BF),
+            pltpu.SemaphoreType.DMA,
             pltpu.SemaphoreType.DMA((96,)),
             pltpu.SemaphoreType.DMA((96,)),
             pltpu.SemaphoreType.DMA((NM,)),
             pltpu.SemaphoreType.DMA((NZ,)),
         ],
-        compiler_params=params(3),
+        compiler_params=params(2, 59),
     )(partial)
 
 
@@ -655,42 +683,27 @@
     return jnp.dot(a, b, preferred_element_type=F32)
 
 
-def rounded(v):
-    return lax.reduce_precision(v, 8, 7)
-
-
-def thirds(v):
-    high = rounded(v)
-    middle = rounded(v - high)
-    return high, middle, v - high - middle
-
-
 def on_device(tokens, assignments, gate_probs, expert_gate, expert_up, expert_down, shared_gate, shared_up, shared_down):
     me = lax.axis_index("expert").astype(F32)
-    split = [part for k in range(2) for part in thirds(gate_probs[:, k : k + 1])]
-    meta = jnp.concatenate([assignments.astype(F32)] + split + [jnp.zeros((BLOCK, 56), F32)], axis=1)
-    tok = jnp.concatenate([tokens, meta.astype(BF)], axis=1)
-    x, gu, down = gather(tok, jnp.concatenate([shared_gate, shared_up], axis=1), shared_down)
+    x, gu, down = gather(tokens.T, assignments.T, gate_probs.T, shared_gate.T, shared_up.T, shared_down)
     wide_x = x.reshape(NZ * NY * PIECE, WIDE)
     info = wide_x[:, FEAT : FEAT + 8].astype(F32)
-    x = wide_x[:, :FEAT]
-    rows = x.shape[0]
+    rows = wide_x.shape[0]
 
     named = (info[:, 0:2] == me).astype(F32)
     hit = named[:, 0] + named[:, 1]
-    weight = named[:, 0] * (info[:, 2] + info[:, 3] + info[:, 4]) + named[:, 1] * (info[:, 5] + info[:, 6] + info[:, 7])
+    weight = named[:, 0] * (info[:, 2] + info[:, 4] + info[:, 6]) + named[:, 1] * (info[:, 3] + info[:, 5] + info[:, 7])
     t = jnp.arange(rows, dtype=jnp.int32)
     group = (t // PIECE) % NY
     before = ((t[:, None] < t[None, :]) & (group[:, None] == group[None, :])).astype(BF)
     rank = dot(hit.astype(BF)[None, :], before)[0]
     slot = jnp.where(hit > 0, group * 16 + rank.astype(jnp.int32), -1)
     place = slot[None, :] == jnp.arange(SLOTS, dtype=jnp.int32)[:, None]
-    picked = dot(place.astype(BF), x).astype(BF)
 
     scale = jnp.sum(place.astype(F32) * weight[None, :], axis=1)
     back = slot[:, None] == jnp.arange(SLOTS, dtype=jnp.int32)[None, :]
     partial = experts(
-        picked,
+        place.astype(BF),
         back.astype(BF),
         scale[:, None],
         wide_x,

time: 161 us -> 155 us (0.963)
  local copies, waits for them, and re-layouts: 9.32 us -> 2.54 us
  Pallas kernels: 145 us -> 148 us
  matrix products: 3.24 us -> 0.31 us
    unnamed x13 -> x0, local copies, waits for them, and re-layouts: 7.01 us -> none
    dot_general x2 -> x1, matrix products: 3.24 us -> 0.31 us  [dot(): return jnp.dot(a, b, preferred_element_type=F32)]
where the time goes in v3:
time: 155 us; the launch traced here: 154 us
  Pallas kernels  148 us (95%)
  other arithmetic  3.77 us (2%)
  local copies, waits for them, and re-layouts  2.54 us (2%)
    pallas_call x1, Pallas kernels, gather(): pl.pallas_call(gather_kernel, name='gather', out_shape=(jax.ShapeDtypeStr...  50.7 us
    pallas_call x1, Pallas kernels, experts(): pl.pallas_call(experts_kernel, name='experts', out_shape=jax.ShapeDtypeSt...  50.7 us
    pallas_call x1, Pallas kernels, reduce_out(): pl.pallas_call(reduce_kernel, name='reduce_out', out_shape=jax.ShapeDtype...  46.3 us

profile of v3, /device:TPU:7, one launch (start us, length us, event | category | flops | bytes accessed | tf_op | source)
XLA Modules:
  0.0 154.3 jit_solution(15366833133161145898)
XLA Ops:
  0.0 50.7 %gather.1 = (bf16[8,4,16,3712]{3,2,1,0:T(8,128)(2,1)}, bf16[8,448,640]{2,1,0:T(8,128)(2,1)}, bf16[8,320,448]{2,1,0:T(8,128)(2,1)}) custom-call(bf16[448,128]{1,0:T(8,128)(2,1)} %bitcast.28, s32[2,128]{1,0:T(2,128)} %bitcast.33, f32[2,128]{1,0:T(2,128)} %bitcast.34, bf16[320,448]{1,0:T(8,128)(2,1)} %bitcast.26, bf16[320,448]{1,0:T(8,128)(2,1)} %bitcast.27, ...), custom_call_target="tpu_custom_call" | custom-call | tf_op jit(solution)/shard_map/gather/pallas_call | solution.py:273
  50.7 0.9 slice_convert_fusion
  51.7 0.6 fusion.7
  52.3 0.2 convert_reduce_fusion
  52.6 0.3 fusion.1
  52.9 0.2 copy.12
  53.1 0.2 select_reduce_fusion
  53.3 0.1 reduce
  53.5 0.1 select_reduce_fusion.1
  53.6 0.7 copy.13.scale_ref
  54.3 0.6 fusion.11.place_ref
  54.9 0.8 fusion.9.back_ref
  55.7 50.7 %experts.1 = bf16[512,3584]{1,0:T(8,128)(2,1)} custom-call(bf16[64,512]{1,0:T(8,128)(2,1)} %fusion.11.place_ref, bf16[512,64]{1,0:T(8,128)(2,1)} %fusion.9.back_ref, f32[64,1]{1,0:T(8,128)} %copy.13.scale_ref, bf16[512,3712]{1,0:T(8,128)(2,1)} %bitcast.22, bf16[3584,640]{1,0:T(8,128)(2,1)} %bitcast.20, bf16[8,320,448]{2,1,0:T(8,128)(2,1)} %get-tuple-element.10.wd_hbm, ...), custom_call_target="tpu_custom_call" | custom-call | tf_op jit(solution)/shard_map/experts/pallas_call | solution.py:462
  106.4 46.3 %reduce_out.1 = bf16[128,448]{1,0:T(8,128)(2,1)} custom-call(bf16[8,4,16,3584]{3,2,1,0:T(8,128)(2,1)} %bitcast.19), custom_call_target="tpu_custom_call" | custom-call | tf_op jit(solution)/shard_map/reduce_out/pallas_call | solution.py:660
  152.7 1.7 %copy.14 = bf16[128,448]{0,1:T(8,128)(2,1)} copy(bf16[128,448]{1,0:T(8,128)(2,1)} %reduce_out.1) | data formatting | bytes 229376 | tf_op jit(solution)/shard_map/reduce_out/pallas_call | solution.py:660
  (5 shorter events, 0.1 us)

commit v4 on v3

--- a/solution.py
+++ b/solution.py
@@ -302,8 +302,8 @@
 
 
 def experts_kernel(
-    place_ref, back_ref, scale_ref, x_hbm, gu_hbm, wd_hbm, eg_hbm, eu_hbm, ed_hbm, out_ref,
-    done, s_ref, shared, value, rows, eg, eu, ed, xs, gu, wd, wide, part, from_pair, from_x, held, send_sem, recv_sem, local_sem, load_sem,
+    x_hbm, gu_hbm, wd_hbm, eg_hbm, eu_hbm, ed_hbm, out_ref,
+    back_ref, scale_ref, done, s_ref, shared, value, rows, eg, eu, ed, xs, gu, wd, wide, part, from_pair, from_x, held, send_sem, recv_sem, local_sem, load_sem,
 ):
     p = Place()
     loads = [
@@ -317,7 +317,28 @@
     neighbours = [p.at("x", 1), p.at("x", -1), p.at("c", 1)]
     barrier = greet(neighbours)
     loads[0].wait()
-    s_ref[...] = dot(place_ref[...], xs[:, :FEAT]).astype(BF)
+    tokens = 4 * BLOCK
+    info = xs[:, FEAT:].astype(F32)
+    me = lax.axis_index("expert").astype(F32)
+
+    def column(k):
+        return info[:, k : k + 1]
+
+    named = [jnp.where(column(k) == me, 1.0, 0.0) for k in range(2)]
+    hit = named[0] + named[1]
+    weight = sum(named[k] * (column(2 + k) + column(4 + k) + column(6 + k)) for k in range(2))
+    t = lax.broadcasted_iota(jnp.int32, (tokens, tokens), 0)
+    u = lax.broadcasted_iota(jnp.int32, (tokens, tokens), 1)
+    same = lax.rem(lax.div(t, PIECE), NY) == lax.rem(lax.div(u, PIECE), NY)
+    before = jnp.where(jnp.logical_and(same, u < t), 1.0, 0.0).astype(BF)
+    rank = dot(before, jnp.broadcast_to(hit, (tokens, 128)).astype(BF))
+    row = lax.broadcasted_iota(jnp.int32, (tokens, 128), 0)
+    lane = lax.broadcasted_iota(jnp.int32, (tokens, 128), 1)
+    slot = rank + (lax.rem(lax.div(row, PIECE), NY) * 16).astype(F32)
+    back = jnp.where(slot == lane.astype(F32), jnp.broadcast_to(hit, (tokens, 128)), 0.0)
+    back_ref[...] = back.astype(BF)
+    scale_ref[...] = jnp.sum((back * weight).T, axis=1, keepdims=True)[:SLOTS]
+    s_ref[...] = dot(back.T[:SLOTS].astype(BF), xs[:, :FEAT]).astype(BF)
     pl.semaphore_wait(barrier, 3)
     wire = Wire(p, send_sem, recv_sem)
     wire.now = 3.0
@@ -446,7 +467,7 @@
 
     def combine(i, carry):
         at = pl.ds(pl.multiple_of(i * ROWS, ROWS), ROWS)
-        done[at, :] = (shared[at, :] + dot(back_ref[at, :], value[...])).astype(BF)
+        done[at, :] = (shared[at, :] + dot(back_ref[at, :SLOTS], value[...])).astype(BF)
         pltpu.make_async_copy(done.at[at, :], out_ref.at[at, :], load_sem.at[i]).start()
         return carry
 
@@ -457,15 +478,17 @@
         pltpu.make_async_copy(done.at[at, :], out_ref.at[at, :], load_sem.at[i]).wait()
 
 
-def experts(place, back, scale, x, gu, wd, eg, eu, ed):
+def experts(x, gu, wd, eg, eu, ed):
     slots = pltpu.VMEM((NX, SLOTS, FEAT), BF)
     return pl.pallas_call(
         experts_kernel,
         name="experts",
         out_shape=jax.ShapeDtypeStruct((4 * BLOCK, FEAT), BF),
-        in_specs=[spec(VM)] * 3 + [spec(ANY)] * 6,
+        in_specs=[spec(ANY)] * 6,
         out_specs=spec(ANY),
         scratch_shapes=[
+            pltpu.VMEM((4 * BLOCK, 128), BF),
+            pltpu.VMEM((SLOTS, 1), F32),
             pltpu.VMEM((4 * BLOCK, FEAT), BF),
             pltpu.VMEM((SLOTS, FEAT), BF),
             pltpu.VMEM((4 * BLOCK, FEAT), F32),
@@ -488,7 +511,7 @@
             pltpu.SemaphoreType.DMA((6,)),
         ],
         compiler_params=params(1, 54),
-    )(place, back, scale, x, gu, wd, eg, eu, ed)
+    )(x, gu, wd, eg, eu, ed)
 
 
 def reduce_kernel(
@@ -675,7 +698,7 @@
             pltpu.SemaphoreType.DMA((NM,)),
             pltpu.SemaphoreType.DMA((NZ,)),
         ],
-        compiler_params=params(2, 59),
+        compiler_params=params(2, 57),
     )(partial)
 
 
@@ -684,29 +707,9 @@
 
 
 def on_device(tokens, assignments, gate_probs, expert_gate, expert_up, expert_down, shared_gate, shared_up, shared_down):
-    me = lax.axis_index("expert").astype(F32)
     x, gu, down = gather(tokens.T, assignments.T, gate_probs.T, shared_gate.T, shared_up.T, shared_down)
-    wide_x = x.reshape(NZ * NY * PIECE, WIDE)
-    info = wide_x[:, FEAT : FEAT + 8].astype(F32)
-    rows = wide_x.shape[0]
-
-    named = (info[:, 0:2] == me).astype(F32)
-    hit = named[:, 0] + named[:, 1]
-    weight = named[:, 0] * (info[:, 2] + info[:, 4] + info[:, 6]) + named[:, 1] * (info[:, 3] + info[:, 5] + info[:, 7])
-    t = jnp.arange(rows, dtype=jnp.int32)
-    group = (t // PIECE) % NY
-    before = ((t[:, None] < t[None, :]) & (group[:, None] == group[None, :])).astype(BF)
-    rank = dot(hit.astype(BF)[None, :], before)[0]
-    slot = jnp.where(hit > 0, group * 16 + rank.astype(jnp.int32), -1)
-    place = slot[None, :] == jnp.arange(SLOTS, dtype=jnp.int32)[:, None]
-
-    scale = jnp.sum(place.astype(F32) * weight[None, :], axis=1)
-    back = slot[:, None] == jnp.arange(SLOTS, dtype=jnp.int32)[None, :]
     partial = experts(
-        place.astype(BF),
-        back.astype(BF),
-        scale[:, None],
-        wide_x,
+        x.reshape(NZ * NY * PIECE, WIDE),
         gu.reshape(FEAT, 640),
         down,
         jnp.swapaxes(expert_gate[0], 0, 1),

time: 155 us -> 149 us (0.961)
  other arithmetic: 3.77 us -> 0 us
    convert_element_type x5 -> x0, other arithmetic: 2.6 us -> none  [the longest x1 0.92 us: on_device(): info = wide_x[:, FEAT:FEAT + 8].astype(F32)]
where the time goes in v4:
time: 149 us
  Pallas kernels  148 us (99%)
  local copies, waits for them, and re-layouts  1.67 us (1%)
    pallas_call x1, Pallas kernels, gather(): pl.pallas_call(gather_kernel, name='gather', out_shape=(jax.ShapeDtypeStr...  50.7 us
    pallas_call x1, Pallas kernels, experts(): pl.pallas_call(experts_kernel, name='experts', out_shape=jax.ShapeDtypeSt...  50.6 us
    pallas_call x1, Pallas kernels, reduce_out(): pl.pallas_call(reduce_kernel, name='reduce_out', out_shape=jax.ShapeDtype...  46.3 us

profile of v4, /device:TPU:7, one launch (start us, length us, event | category | flops | bytes accessed | tf_op | source)
XLA Modules:
  0.0 149.2 jit_solution(4931798036836051155)
XLA Ops:
  0.0 50.7 %gather.1 = (bf16[8,4,16,3712]{3,2,1,0:T(8,128)(2,1)}, bf16[8,448,640]{2,1,0:T(8,128)(2,1)}, bf16[8,320,448]{2,1,0:T(8,128)(2,1)}) custom-call(bf16[448,128]{1,0:T(8,128)(2,1)} %bitcast.23, s32[2,128]{1,0:T(2,128)} %bitcast.24, f32[2,128]{1,0:T(2,128)} %bitcast.25, bf16[320,448]{1,0:T(8,128)(2,1)} %bitcast.21, bf16[320,448]{1,0:T(8,128)(2,1)} %bitcast.22, ...), custom_call_target="tpu_custom_call" | custom-call | tf_op jit(solution)/shard_map/gather/pallas_call | solution.py:273
  50.7 50.6 %experts.1 = bf16[512,3584]{1,0:T(8,128)(2,1)} custom-call(bf16[512,3712]{1,0:T(8,128)(2,1)} %bitcast.17, bf16[3584,640]{1,0:T(8,128)(2,1)} %bitcast.16, bf16[8,320,448]{2,1,0:T(8,128)(2,1)} %get-tuple-element.10.wd_hbm, bf16[320,3584]{1,0:T(8,128)(2,1)} %bitcast.18, bf16[320,3584]{1,0:T(8,128)(2,1)} %bitcast.19, bf16[320,3584]{1,0:T(8,128)(2,1)} %bitcast.20), custom_call_target="tpu_custom_call" | custom-call | tf_op jit(solution)/shard_map/experts/pallas_call | solution.py:483
  101.3 46.3 %reduce_out.1 = bf16[128,448]{1,0:T(8,128)(2,1)} custom-call(bf16[8,4,16,3584]{3,2,1,0:T(8,128)(2,1)} %bitcast.15), custom_call_target="tpu_custom_call" | custom-call | tf_op jit(solution)/shard_map/reduce_out/pallas_call | solution.py:683
  147.6 1.7 %copy.10 = bf16[128,448]{0,1:T(8,128)(2,1)} copy(bf16[128,448]{1,0:T(8,128)(2,1)} %reduce_out.1) | data formatting | bytes 229376 | tf_op jit(solution)/shard_map/reduce_out/pallas_call | solution.py:683
